TPU v7x, 32 devices: a whole 2x2x4 slice. The times are simulated.
32 devices in a mesh: groups: 1, row: 16 (over z, y, core), col: 2 (over x).
Axes of the slice: x: 2, y: 2, z: 4, core: 2. Of those that a mesh axis runs over, the one named last changes fastest.
Arguments:
- pair_grid: bfloat16 [256, 256, 128], P(('groups', 'row'), 'col'), may hold values from -6 to 6
- alignment_pool: bfloat16 [256, 256, 64], P('groups', 'row'), may hold values from -6 to 6
- sample_index: int32 [64], P('groups'), may hold values from 0 to 255
- token_mask: int32 [256], P('groups'), may hold values 0 or 1
- outer_proj: bfloat16 [64, 64], replicated, may hold values from -0.75 to 0.75
- outer_mix: bfloat16 [1024, 128], replicated, may hold values from -0.375 to 0.375
- pair_logit: bfloat16 [128, 8], replicated, may hold values from -1 to 1
- average_proj: bfloat16 [64, 512], replicated, may hold values from -0.75 to 0.75
- average_mix: bfloat16 [256, 64], replicated, may hold values from -0.75 to 0.75
- triangle_proj: bfloat16 [128, 640], replicated, may hold values from -0.5 to 0.5
- triangle_mix: bfloat16 [128, 128], replicated, may hold values from -0.5 to 0.5
- transition_up: bfloat16 [128, 1024], replicated, may hold values from -0.5 to 0.5
- transition_down: bfloat16 [512, 128], replicated, may hold values from -0.25 to 0.25
Outputs:
- pair_next: bfloat16 [256, 256, 128], P(('groups', 'row'), 'col')
- alignment_next: bfloat16 [64, 256, 64], P('groups', 'row')
Inputs may be any that keep to these rules, and one draw needn't show every extreme that they name: `sample_index`: indices into the first dimension of alignment_pool; they may repeat. `token_mask`: 1 marks a real residue, 0 a padded one.
All inputs are finite; a program needn't handle non-finite values.
Results may differ from a plain program's by a relative error of at most 0.008.
Values may be sent and summed in bfloat16 or wider, within the bound.
A program may use at most 64 MiB of HBM per device.

v0:
```python
import jax
import jax.numpy as jnp
from jax import lax
from jax.sharding import PartitionSpec as P

epsilon = 1e-05


def normalize(values, channel_dim):
    values = values.astype(jnp.float32)
    centred = values - jnp.mean(values, axis=channel_dim, keepdims=True)
    spread = jnp.mean(centred * centred, axis=channel_dim, keepdims=True)
    return centred / jnp.sqrt(spread + epsilon)


def triangle_product(exchanged, n_row, n_col):
    left_part = exchanged[0]
    right_part = exchanged[1]
    item_count = left_part.shape[2]
    tok_row = left_part.shape[3]
    tok_col = left_part.shape[4]
    product = jnp.einsum(
        "ruxiq,suxjq->xrisj", left_part, right_part, preferred_element_type=jnp.float32
    )
    product = product.reshape(item_count, n_row, tok_row, n_col, tok_col)
    return product.transpose(1, 3, 0, 2, 4).astype(jnp.bfloat16)


def on_device(
    pair_grid,
    alignment_pool,
    sample_index,
    token_mask,
    outer_proj,
    outer_mix,
    pair_logit,
    average_proj,
    average_mix,
    triangle_proj,
    triangle_mix,
    transition_up,
    transition_down,
):
    n_row = lax.axis_size("row")
    n_col = lax.axis_size("col")
    tok_row = pair_grid.shape[0]
    tok_col = pair_grid.shape[1]
    pair_width = pair_grid.shape[2]
    samples = sample_index.shape[0]
    align_width = alignment_pool.shape[2]
    outer_width = outer_proj.shape[1] // 2
    head_count = pair_logit.shape[1]
    head_total = average_proj.shape[1] // 2
    head_dim = head_total // head_count
    inner_width = transition_down.shape[0]
    row_start = lax.axis_index("row") * tok_row
    column_start = lax.axis_index("col") * tok_col
    alignments = jnp.take(alignment_pool, sample_index, axis=0)
    align_norm = normalize(alignments, 2).astype(jnp.bfloat16)
    align_rows = align_norm.reshape(samples, tok_row * align_width)
    gathered = lax.all_gather(align_rows, "row", axis=1, tiled=True)
    column_flat = lax.dynamic_slice_in_dim(
        gathered, column_start * align_width, tok_col * align_width, 1
    )
    column_norm = column_flat.reshape(samples, tok_col, align_width)
    row_factor = jnp.dot(
        align_norm, outer_proj[:, :outer_width], preferred_element_type=jnp.float32
    ).astype(jnp.bfloat16)
    column_factor = jnp.dot(
        column_norm, outer_proj[:, outer_width:], preferred_element_type=jnp.float32
    ).astype(jnp.bfloat16)
    column_rows = column_factor.reshape(samples, tok_col * outer_width)
    block_rows = 8
    block_count = tok_row // block_rows
    row_blocks = row_factor.reshape(samples, block_count, block_rows * outer_width).transpose(
        1, 0, 2
    )
    pair_blocks = pair_grid.reshape(block_count, block_rows, tok_col, pair_width)

    def outer_step(operands):
        left_block, pair_block = operands
        outer_sum = lax.dot_general(
            left_block, column_rows, (((0,), (0,)), ((), ())), preferred_element_type=jnp.float32
        )
        outer_sum = outer_sum.reshape(block_rows, outer_width, tok_col, outer_width).transpose(
            0, 2, 1, 3
        )
        outer_mean = (
            (outer_sum * (1.0 / samples))
            .astype(jnp.bfloat16)
            .reshape(block_rows * tok_col, outer_width * outer_width)
        )
        update = jnp.dot(outer_mean, outer_mix, preferred_element_type=jnp.float32).reshape(
            block_rows, tok_col, pair_width
        )
        return (pair_block.astype(jnp.float32) + update).astype(jnp.bfloat16)

    pair_one = lax.map(outer_step, (row_blocks, pair_blocks)).reshape(tok_row, tok_col, pair_width)
    pair_norm = normalize(pair_one, 2).astype(jnp.bfloat16)
    value_weight = average_proj[:, :head_total].reshape(align_width, head_count, head_dim)
    gate_weight = average_proj[:, head_total:].reshape(align_width, head_count, head_dim)
    mix_weight = average_mix.reshape(head_count, head_dim, align_width)
    scores = lax.dot_general(
        pair_logit, pair_norm, (((0,), (2,)), ((), ())), preferred_element_type=jnp.float32
    )
    weights = jnp.exp(scores)
    partial_total = jnp.sum(weights, axis=2)
    weights_low = weights.astype(jnp.bfloat16)
    column_values = jnp.einsum(
        "sjm,mhc->hjsc", column_norm, value_weight, preferred_element_type=jnp.float32
    )
    column_values = column_values.astype(jnp.bfloat16).reshape(
        head_count, tok_col, samples * head_dim
    )
    partial_sum = jnp.einsum(
        "hij,hjk->hik", weights_low, column_values, preferred_element_type=jnp.float32
    )
    weighted, totals = (
        lax.psum(partial_sum.astype(jnp.bfloat16), "col").astype(jnp.float32),
        lax.psum(partial_total.astype(jnp.bfloat16), "col").astype(jnp.float32),
    )
    gate_values = jax.nn.sigmoid(
        jnp.einsum("sim,mhc->hisc", align_norm, gate_weight, preferred_element_type=jnp.float32)
    )
    weighted = weighted.reshape(head_count, tok_row, samples, head_dim)
    averaged = (gate_values * weighted / totals[:, :, None, None]).astype(jnp.bfloat16)
    align_update = jnp.einsum(
        "hisc,hcm->sim", averaged, mix_weight, preferred_element_type=jnp.float32
    )
    alignment_next = (alignments.astype(jnp.float32) + align_update).astype(jnp.bfloat16)
    flat_norm = pair_norm.reshape(tok_row * tok_col, pair_width)
    projected = lax.dot_general(
        triangle_proj[:, : 4 * pair_width],
        flat_norm,
        (((0,), (1,)), ((), ())),
        preferred_element_type=jnp.float32,
    )
    projected = projected.reshape(4, pair_width, tok_row, tok_col)
    row_mask = lax.dynamic_slice_in_dim(token_mask, row_start, tok_row, 0).astype(jnp.float32)
    column_mask = lax.dynamic_slice_in_dim(token_mask, column_start, tok_col, 0).astype(jnp.float32)
    pair_mask = row_mask[:, None] * column_mask[None, :]
    left_side = jax.nn.sigmoid(projected[0]) * projected[1] * pair_mask
    right_side = jax.nn.sigmoid(projected[2]) * projected[3] * pair_mask
    factors = jnp.stack([left_side, right_side]).astype(jnp.bfloat16)
    group_size = pair_width // (n_row * n_col)
    grouped = factors.reshape(2, n_row * n_col, group_size, tok_row, tok_col)
    received = lax.all_to_all(grouped, ("row", "col"), split_axis=1, concat_axis=1, tiled=True)
    arranged = received.reshape(2, n_row, n_col, received.shape[2], tok_row, tok_col)
    result = triangle_product(arranged, n_row, n_col)
    flat_result = result.reshape(n_row * n_col, result.shape[2], tok_row, tok_col)
    product = lax.all_to_all(flat_result, ("row", "col"), split_axis=0, concat_axis=0, tiled=True)
    product = product.reshape(pair_width, tok_row, tok_col)
    product_norm = normalize(product, 0).astype(jnp.bfloat16).reshape(pair_width, tok_row * tok_col)
    mixed = lax.dot_general(
        product_norm, triangle_mix, (((0,), (0,)), ((), ())), preferred_element_type=jnp.float32
    )
    gate_out = jax.nn.sigmoid(
        jnp.dot(flat_norm, triangle_proj[:, 4 * pair_width :], preferred_element_type=jnp.float32)
    )
    pair_two = (
        pair_one.reshape(tok_row * tok_col, pair_width).astype(jnp.float32) + gate_out * mixed
    ).astype(jnp.bfloat16)
    tail_rows = pair_two.reshape(block_count, block_rows * tok_col, pair_width)

    def transition_step(rows_block):
        normed = normalize(rows_block, 1).astype(jnp.bfloat16)
        expanded = jnp.dot(normed, transition_up, preferred_element_type=jnp.float32)
        hidden = (jax.nn.silu(expanded[:, :inner_width]) * expanded[:, inner_width:]).astype(
            jnp.bfloat16
        )
        return (
            rows_block.astype(jnp.float32)
            + jnp.dot(hidden, transition_down, preferred_element_type=jnp.float32)
        ).astype(jnp.bfloat16)

    pair_next = lax.map(transition_step, tail_rows).reshape(tok_row, tok_col, pair_width)
    return (pair_next, alignment_next)


def solution(mesh):
    in_specs = (
        P(("groups", "row"), "col", None),
        P("groups", "row", None),
        P("groups"),
        P("groups"),
        P(),
        P(),
        P(),
        P(),
        P(),
        P(),
        P(),
        P(),
        P(),
    )
    out_specs = (P(("groups", "row"), "col", None), P("groups", "row", None))
    return jax.shard_map(
        on_device, mesh=mesh, in_specs=in_specs, out_specs=out_specs, check_vma=False
    )
```

profile of v0, /device:TPU:0, one launch (start us, length us, event | category | flops | bytes accessed | tf_op | source)
XLA Modules:
  0.0 163.6 jit_solution(2614358065298384016)
XLA Ops:
  8.5 2.0 %copy.82 = bf16[256,16,64]{2,1,0:T(8,128)(2,1)S(1)} copy(bf16[256,16,64]{0,2,1:T(8,128)(2,1)} %param.18) | data formatting | bytes 1048576 | tf_op args[1]
  14.1 1.2 convolution_convert_fusion.2
  15.3 42.9 %all-gather.2.cloned.1.call-done = bf16[64,16384]{1,0:T(8,128)(2,1)} async-done(((bf16[64,1024]{1,0:T(8,128)(2,1)}), bf16[64,16384]{1,0:T(8,128)(2,1)}) %all-gather.2.cloned.1.call-update) | async-done | bytes 2097168 | tf_op jit(solution)/shard_map/all_gather | solution.py:61
  58.2 2.3 %constant_dynamic-slice_fusion.1 = bf16[64,8192]{1,0:T(8,128)(2,1)} fusion(bf16[64,16384]{1,0:T(8,128)(2,1)} %all-gather.2.cloned.1.call-done, s32[]{:T(128)S(6)} %select_n.24), kind=kLoop, calls=%fused_computation.116 | loop fusion | bytes 2097156 | tf_op jit(solution)/shard_map/dynamic_slice | solution.py:62
  60.5 3.3 %reshape.294 = bf16[64,128,64]{2,1,0:T(8,128)(2,1)S(1)} reshape(bf16[64,8192]{1,0:T(8,128)(2,1)} %constant_dynamic-slice_fusion.1) | data formatting | bytes 2097152 | tf_op jit(solution)/shard_map/reshape | solution.py:65
  63.8 1.3 copy-done.1
  65.1 0.9 convolution_convert_fusion.1
  66.0 1.7 %copy.89 = bf16[64,128,32]{0,2,1:T(8,128)(2,1)S(1)} copy(bf16[64,128,32]{1,2,0:T(8,128)(2,1)S(1)} %convolution_convert_fusion.1) | data formatting | bytes 1048576 | tf_op jit(solution)/shard_map/convert_element_type | solution.py:71
  67.7 9.3 %while.20 = (s32[]{:T(128)}, bf16[2,8,128,128]{3,2,1,0:T(8,128)(2,1)S(1)}, bf16[2,8,128,128]{3,2,1,0:T(8,128)(2,1)}, bf16[2,64,256]{1,2,0:T(8,128)(2,1)}, bf16[6...) while((s32[]{:T(128)}, bf16[2,8,128,128]{3,2,1,0:T(8,128)(2,1)S(1)}, ...), condition=%wide.region_3.4_spmd, body=%wide.region_2.3_spmd.sunk | while | flops 405143552 | bytes 13992077 | solution.py:98
  68.6 1.1 copy.148
  73.2 1.1 copy.148
  80.0 1.6 slice_multiply_fusion.2
  82.1 1.6 copy.91
  84.2 1.2 copy.92
  85.5 3.4 %all-to-all-start = ((bf16[2,32,4,16,128]{4,3,2,0,1:T(8,128)(2,1)}), bf16[2,32,4,16,128]{4,3,2,0,1:T(8,128)(2,1)}, u32[]{:S(2)}, u32[]{:S(2)}) async-start(bf16[2,32,4,16,128]{4,3,2,0,1:T(8,128)(2,1)} %copy.92), calls=%async_computation | async-start | bytes 2097152 | tf_op jit(solution)/shard_map/all_to_all | solution.py:147
  89.4 1.3 convert_bitcast_fusion.1
  92.5 1.2 convolution_convert_fusion
  93.7 1.6 %reshape.302 = bf16[8,16,64,32]{3,2,1,0:T(8,128)(2,1)S(1)} reshape(bf16[8,16,2048]{2,1,0:T(8,128)(2,1)S(1)} %convolution_convert_fusion) | data formatting | bytes 1048576 | tf_op jit(solution)/shard_map/reshape | solution.py:125
  95.3 1.6 copy.103
  97.0 18.1 %all-to-all-done = bf16[2,32,4,16,128]{4,3,2,0,1:T(8,128)(2,1)} async-done(((bf16[2,32,4,16,128]{4,3,2,0,1:T(8,128)(2,1)}), bf16[2,32,4,16,128]{4,3,2,0,1:T(8,128)(2,1)}, u32[]{:S(2)}, u32[]{:S(2)}) %all-to-all-start) | async-done | bytes 1048608 | tf_op jit(solution)/shard_map/all_to_all | solution.py:147
  115.1 1.4 fusion.76
  116.6 1.3 bitcast_convert_fusion
  117.9 3.0 %copy.95 = bf16[4,16,16,16,16]{4,3,2,1,0:T(8,128)(2,1)} copy(bf16[4,16,16,16,16]{4,2,3,1,0:T(8,128)(2,1)S(1)} %bitcast_convert_fusion) | data formatting | bytes 1048576 | tf_op jit(solution)/shard_map/convert_element_type | solution.py:26
  120.9 5.8 %convert_element_type.146 = bf16[4,16,16,2,128]{4,3,2,1,0:T(2,128)(2,1)S(1)} reshape(bf16[4,16,16,16,16]{4,3,2,1,0:T(8,128)(2,1)} %copy.95) | data formatting | bytes 1048576 | tf_op jit(solution)/shard_map/convert_element_type | solution.py:26
  126.7 0.9 copy.96
  127.7 3.6 %all-to-all-start.1 = ((bf16[32,4,16,128]{3,2,1,0:T(8,128)(2,1)}), bf16[32,4,16,128]{3,2,1,0:T(8,128)(2,1)S(1)}, u32[]{:S(2)}, u32[]{:S(2)}) async-start(bf16[32,4,16,128]{3,2,1,0:T(8,128)(2,1)} %bitcast.34), calls=%async_computation.1 | async-start | bytes 1048576 | tf_op jit(solution)/shard_map/all_to_all | solution.py:151
  131.6 8.5 %psum.15 = bf16[8,16]{1,0:T(8,128)(2,1)S(1)} all-reduce(bf16[8,16]{1,0:T(8,128)(2,1)S(1)} %copy.104), channel_id=1, replica_groups=mesh['groups'=1,'row'=16,'col'=2] {'col'}, use_global_device_ids=true, to_apply=%region_14.15 | all-reduce | flops 128 | bytes 512 | tf_op jit(solution)/shard_map/psum | solution.py:120
  140.2 2.1 %fusion.26 = f32[2048,128]{1,0:T(8,128)} fusion(bf16[2048,128]{1,0:T(8,128)(2,1)S(1)} %copy-done.5, bf16[128,640]{1,0:T(8,128)(2,1)} %param.26), kind=kOutput, calls=%fused_computation.39 | convolution fusion | flops 67895296 | bytes 1605632 | tf_op jit(solution)/shard_map/dot_general | solution.py:158
  142.3 3.7 %all-reduce.2.cloned.1.call-done = bf16[8,16,64,32]{2,3,1,0:T(8,128)(2,1)} async-done(((bf16[8,16,64,32]{2,3,1,0:T(8,128)(2,1)}), bf16[8,16,64,32]{2,3,1,0:T(8,128)(2,1)}) %all-reduce.2.cloned.1.call-update) | async-done | bytes 524304 | tf_op jit(solution)/shard_map/psum | solution.py:119
  146.1 2.5 %fusion.32 = bf16[64,16,64]{2,0,1:T(8,128)(2,1)S(1)} fusion(bf16[8,32,64,1]{2,1,3,0:T(8,128)(2,1)S(1)} %bitcast.239, bf16[8,16,64,32]{2,3,1,0:T(8,128)(2,1)} %all-reduce.2.cloned.1.call-done, bf16[64,8,32,1]{0,2,3,1:T(8,128)(2,1)S(1)} %bitcast.238, f32[8,16]{1,0:T(8,128)S(1)} %convert_element_type.161, f32[64,16]{0,1:T(8,128)S(1)} %add_sqrt_fusion.2, ...), kind=kOutput, calls=%fused_computation.49 | convolution fusion | flops 69533696 | bytes 860736 | tf_op jit(solution)/shard_map/hisc,hcm->sim/dot_general | solution.py:127
  149.9 1.8 %fusion.27 = bf16[2048,128]{1,0:T(8,128)(2,1)S(1)} fusion(f32[2048,128]{1,0:T(8,128)} %fusion.26, bf16[128,128]{1,0:T(8,128)(2,1)S(1)} %copy-done, f32[16,8,16,128]{3,2,1,0:T(8,128)S(1)} %bitcast_convert_fusion.1, f32[2048]{0:T(1024)S(1)} %sqrt_bitcast_fusion, f32[2048]{0:T(1024)S(1)} %get-tuple-element.106, bf16[2048,128]{1,0:T(8,128)(2,1)S(1)} %bitcast.227), kind=kOutput, calls=%fused_computation.41 | convolution fusion | flops 68943872 | bytes 3194880 | tf_op jit(solution)/shard_map/dot_general | solution.py:154
  151.8 4.2 %while.21 = (s32[]{:T(128)}, bf16[2,1024,128]{2,1,0:T(8,128)(2,1)S(1)}, bf16[2,1024,128]{2,1,0:T(8,128)(2,1)S(1)}, bf16[128,1024]{1,0:T(8,128)(2,1)S(1)}, bf16[512,128]{1,0:T(8,128)(2,1)S(1)}, /*index=5*/s32[]{:T(128)}) while((s32[]{:T(128)}, bf16[2,1024,128]{2,1,0:T(8,128)(2,1)S(1)}, bf16[2,1024,128]{2,1,0:T(8,128)(2,1)S(1)}, ...), condition=%wide.region_11.12_spmd, body=%wide.region_8.11_spmd.sunk | while | flops 407503872 | bytes 10129493 | solution.py:176
  (109 shorter events, 24.8 us)
Async XLA Ops:
  7.2 142.7 %copy-start = (bf16[128,128]{1,0:T(8,128)(2,1)S(1)}, bf16[128,128]{1,0:T(8,128)(2,1)}, u32[]{:S(2)}) copy-start(bf16[128,128]{1,0:T(8,128)(2,1)} %param.27) | copy-start | bytes 98308
  7.2 51.0 %all-gather.2.cloned.1.call-start = ((), (), s32[]{:S(2)}) async-start(), calls=%async_computation.2 | async-start | bytes 2228224 | tf_op jit(solution)/shard_map/all_gather | solution.py:61
  11.9 2.0 %copy-start.14 = (s32[256]{0:T(256)S(1)}, s32[256]{0:T(256)}, u32[]{:S(2)}) copy-start(s32[256]{0:T(256)} %param.20) | copy-start | bytes 3076
  11.9 2.2 %copy-start.9 = (bf16[64,64]{1,0:T(8,128)(2,1)S(1)}, bf16[64,64]{1,0:T(8,128)(2,1)}, u32[]{:S(2)}) copy-start(bf16[64,64]{1,0:T(8,128)(2,1)} %param.21) | copy-start | bytes 24580
  63.8 1.3 copy-start.1
  70.4 1.0 copy-start.11
  70.4 1.1 copy-start.12
  75.0 1.0 copy-start.11
  75.0 1.1 copy-start.12
  77.0 2.3 %copy-start.6 = (bf16[128,640]{1,0:T(8,128)(2,1)S(1)}, bf16[128,640]{1,0:T(8,128)(2,1)}, u32[]{:S(2)}) copy-start(bf16[128,640]{1,0:T(8,128)(2,1)} %param.26) | copy-start | bytes 491524
  78.5 0.8 copy-start.4
  84.2 5.0 %copy-start.7 = (bf16[64,512]{1,0:T(8,128)(2,1)S(1)}, bf16[64,512]{1,0:T(8,128)(2,1)}, u32[]{:S(2)}) copy-start(bf16[64,512]{1,0:T(8,128)(2,1)} %param.24) | copy-start | bytes 196612
  84.2 5.1 %copy-start.2 = (bf16[64,128,64]{2,1,0:T(8,128)(2,1)S(1)}, bf16[64,128,64]{2,1,0:T(8,128)(2,1)}, u32[]{:S(2)}) copy-start(bf16[64,128,64]{2,1,0:T(8,128)(2,1)} %copy-done.1) | copy-start | bytes 3145732
  85.5 29.6 %all-to-all-start = ((bf16[2,32,4,16,128]{4,3,2,0,1:T(8,128)(2,1)}), bf16[2,32,4,16,128]{4,3,2,0,1:T(8,128)(2,1)}, u32[]{:S(2)}, u32[]{:S(2)}) async-start(bf16[2,32,4,16,128]{4,3,2,0,1:T(8,128)(2,1)} %copy.92), calls=%async_computation | async-start | bytes 2097152 | tf_op jit(solution)/shard_map/all_to_all | solution.py:147
  88.9 57.1 %all-reduce.2.cloned.1.call-start = ((), (), s32[]{:S(2)}) async-start(), calls=%async_computation.3 | async-start | bytes 2097152 | tf_op jit(solution)/shard_map/psum | solution.py:119
  90.6 1.5 copy-start.10
  126.7 4.7 %copy-start.8 = (bf16[256,64]{0,1:T(8,128)(2,1)S(1)}, bf16[256,64]{0,1:T(8,128)(2,1)}, u32[]{:S(2)}) copy-start(bf16[256,64]{0,1:T(8,128)(2,1)} %param.25) | copy-start | bytes 98308
  126.7 13.5 %copy-start.5 = (bf16[2048,128]{1,0:T(8,128)(2,1)S(1)}, bf16[2048,128]{1,0:T(8,128)(2,1)}, u32[]{:S(2)}) copy-start(bf16[2048,128]{1,0:T(8,128)(2,1)} %copy-done.4) | copy-start | bytes 1572868
  127.7 21.7 %all-to-all-start.1 = ((bf16[32,4,16,128]{3,2,1,0:T(8,128)(2,1)}), bf16[32,4,16,128]{3,2,1,0:T(8,128)(2,1)S(1)}, u32[]{:S(2)}, u32[]{:S(2)}) async-start(bf16[32,4,16,128]{3,2,1,0:T(8,128)(2,1)} %bitcast.34), calls=%async_computation.1 | async-start | bytes 1048576 | tf_op jit(solution)/shard_map/all_to_all | solution.py:151
  149.9 1.8 %copy-start.3 = (bf16[128,1024]{1,0:T(8,128)(2,1)S(1)}, bf16[128,1024]{1,0:T(8,128)(2,1)}, u32[]{:S(2)}) copy-start(bf16[128,1024]{1,0:T(8,128)(2,1)} %param.28) | copy-start | bytes 786436
  149.9 1.8 %copy-start.13 = (bf16[512,128]{1,0:T(8,128)(2,1)S(1)}, bf16[512,128]{1,0:T(8,128)(2,1)}, u32[]{:S(2)}) copy-start(bf16[512,128]{1,0:T(8,128)(2,1)} %param.29) | copy-start | bytes 393220
  156.0 0.8 copy-start.15
Sparse Core Ops, SparseCore 0:
  14.0 44.1 all-gather.1
  97.1 48.9 all-reduce.1
where the time goes:
time: 165 us; the launch traced here: 164 us
  waiting for transfers between devices  64.8 us (39%)
  local copies, waits for them, and re-layouts  40.2 us (24%)
  matrix products  19.5 us (12%)
  between operations  14.5 us (9%)
  blocking collectives  8.55 us (5%)
  other arithmetic  8.53 us (5%)
  starting transfers between devices  7.39 us (4%)
    all_gather x1, waiting for transfers between devices, on_device(): gathered = lax.all_gather(align_rows, 'row', axis=1, tiled=True)  42.9 us
    all_to_all x1, waiting for transfers between devices, on_device(): lax.all_to_all(grouped, ('row', 'col'), split_axis=1, concat_axis=1, tile...  18.1 us
    convert_element_type x3, local copies, waits for them, and re-layouts, triangle_product(): return product.transpose(1, 3, 0, 2, 4).astype(jnp.bfloat16)  9.76 us
    psum x1, blocking collectives, on_device(): lax.psum(partial_total.astype(jnp.bfloat16), 'col').astype(jnp.float32)  8.55 us
    unnamed x36, local copies, waits for them, and re-layouts  6.61 us
    psum x1, waiting for transfers between devices, on_device(): lax.psum(partial_sum.astype(jnp.bfloat16), 'col').astype(jnp.float32)  3.71 us
    all_to_all x1, starting transfers between devices, on_device(): lax.all_to_all(flat_result, ('row', 'col'), split_axis=0, concat_axis=0,...  3.64 us
    all_to_all x1, starting transfers between devices, on_device(): lax.all_to_all(grouped, ('row', 'col'), split_axis=1, concat_axis=1, tile...  3.45 us
  transfers between devices with their start and end apart: 4, of which 3 were waited for; matrix products, arithmetic and copies ran while one was open for 17% of the time, Pallas kernels for 0%

commit v1 on v0

--- a/solution.py
+++ b/solution.py
@@ -1,6 +1,10 @@
+import functools
+
 import jax
 import jax.numpy as jnp
 from jax import lax
+from jax.experimental import pallas as pl
+from jax.experimental.pallas import tpu as pltpu
 from jax.sharding import PartitionSpec as P
 
 epsilon = 1e-05
@@ -13,17 +17,154 @@
     return centred / jnp.sqrt(spread + epsilon)
 
 
-def triangle_product(exchanged, n_row, n_col):
-    left_part = exchanged[0]
-    right_part = exchanged[1]
-    item_count = left_part.shape[2]
-    tok_row = left_part.shape[3]
-    tok_col = left_part.shape[4]
-    product = jnp.einsum(
-        "ruxiq,suxjq->xrisj", left_part, right_part, preferred_element_type=jnp.float32
-    )
-    product = product.reshape(item_count, n_row, tok_row, n_col, tok_col)
-    return product.transpose(1, 3, 0, 2, 4).astype(jnp.bfloat16)
+def gather_kernel(n_row, n_col, block_ref, out_ref, own_sem, send_sems, far_sems, recv_sems):
+    span = n_row // n_col
+    row = lax.axis_index("row")
+    col = lax.axis_index("col")
+    band = row // span
+    place = lax.rem(row, span)
+    parity = lax.rem(place, 2)
+    base = band * span
+    twin_place = place + 1 - 2 * parity
+    is_source = band == col
+    half = span // 2
+
+    def other_band(k):
+        return lax.rem(band + k, n_col) * span + place
+
+    def peer_place(k):
+        return lax.rem(place + 2 * k, span)
+
+    barrier = pltpu.get_barrier_semaphore()
+    for k in range(1, n_col):
+        pl.semaphore_signal(barrier, inc=1, device_id={"row": other_band(k)})
+    pl.semaphore_signal(barrier, inc=1, device_id={"row": base + twin_place})
+    for k in range(1, half):
+        pl.semaphore_signal(barrier, inc=1, device_id={"row": base + peer_place(k)})
+    pl.semaphore_wait(barrier, n_col - 1 + half)
+
+    def push(source, slot, sem, recv, target):
+        return pltpu.make_async_remote_copy(
+            src_ref=source,
+            dst_ref=out_ref.at[slot],
+            send_sem=sem,
+            recv_sem=recv,
+            device_id={"row": target},
+        )
+
+    def far(k):
+        return push(block_ref, place, far_sems.at[k - 1], recv_sems.at[place], other_band(k))
+
+    @pl.when(is_source)
+    def _():
+        for k in range(1, n_col):
+            far(k).start()
+        own = pltpu.make_async_copy(block_ref, out_ref.at[place], own_sem)
+        own.start()
+        own.wait()
+
+    @pl.when(jnp.logical_not(is_source))
+    def _():
+        push(block_ref, place, own_sem, recv_sems.at[place], base + twin_place).wait_recv()
+
+    mine = out_ref.at[place]
+    near = [
+        push(mine, place, send_sems.at[k - 1], recv_sems.at[place], base + peer_place(k))
+        for k in range(1, half)
+    ]
+    near.append(push(mine, place, send_sems.at[half - 1], recv_sems.at[place], base + twin_place))
+    for copy in near:
+        copy.start()
+    for k in range(1, half):
+        came = lax.rem(place - 2 * k + span, span)
+        push(mine, came, own_sem, recv_sems.at[came], base + twin_place).wait_recv()
+        onward = push(
+            out_ref.at[came],
+            came,
+            send_sems.at[half - 1 + k],
+            recv_sems.at[came],
+            base + twin_place,
+        )
+        onward.start()
+        near.append(onward)
+    for k in range(half):
+        came = lax.rem(twin_place + 2 * k, span)
+        push(mine, came, own_sem, recv_sems.at[came], base + twin_place).wait_recv()
+    for copy in near:
+        copy.wait_send()
+
+    @pl.when(is_source)
+    def _():
+        for k in range(1, n_col):
+            far(k).wait_send()
+
+
+def gather_blocks(block, collective_id):
+    n_row = lax.axis_size("row")
+    n_col = lax.axis_size("col")
+    span = n_row // n_col
+    return pl.pallas_call(
+        functools.partial(gather_kernel, n_row, n_col),
+        out_shape=jax.ShapeDtypeStruct((span,) + block.shape, block.dtype),
+        in_specs=[pl.BlockSpec(memory_space=pltpu.VMEM)],
+        out_specs=pl.BlockSpec(memory_space=pltpu.VMEM),
+        scratch_shapes=[
+            pltpu.SemaphoreType.DMA,
+            pltpu.SemaphoreType.DMA((span,)),
+            pltpu.SemaphoreType.DMA((max(n_col - 1, 1),)),
+            pltpu.SemaphoreType.DMA((span,)),
+        ],
+        compiler_params=pltpu.CompilerParams(
+            collective_id=collective_id, has_side_effects=True
+        ),
+        name=f"gather_{collective_id}",
+    )(block)
+
+
+def sum_columns(values, wire_dtype):
+    n_col = lax.axis_size("col")
+    total = values
+    sent = values.astype(wire_dtype)
+    for shift in range(1, n_col):
+        pairs = [(k, (k + shift) % n_col) for k in range(n_col)]
+        total = total + lax.ppermute(sent, "col", pairs).astype(jnp.float32)
+    return total
+
+
+def product_kernel(n_row, n_col, tok_row, tok_col, received_ref, out_ref, left_ref, right_ref):
+    for r in range(n_row):
+        for u in range(n_col):
+            rows = slice(r * tok_row, (r + 1) * tok_row)
+            lanes = slice(u * tok_col, (u + 1) * tok_col)
+            left_ref[rows, lanes] = received_ref[0, r * n_col + u, 0]
+            right_ref[rows, lanes] = received_ref[1, r * n_col + u, 0]
+    result = lax.dot_general(
+        left_ref[...], right_ref[...], (((1,), (1,)), ((), ())), preferred_element_type=jnp.float32
+    ).astype(jnp.bfloat16)
+    for r in range(n_row):
+        for u in range(n_col):
+            rows = slice(r * tok_row, (r + 1) * tok_row)
+            lanes = slice(u * tok_col, (u + 1) * tok_col)
+            out_ref[r * n_col + u, 0] = result[rows, lanes]
+
+
+def triangle_product(received, n_row, n_col):
+    _, devices, items, tok_row, tok_col = received.shape
+    length = n_row * tok_row
+    return pl.pallas_call(
+        functools.partial(product_kernel, n_row, n_col, tok_row, tok_col),
+        grid=(items,),
+        out_shape=jax.ShapeDtypeStruct((devices, items, tok_row, tok_col), jnp.bfloat16),
+        in_specs=[
+            pl.BlockSpec((2, devices, 1, tok_row, tok_col), lambda c: (0, 0, c, 0, 0))
+        ],
+        out_specs=pl.BlockSpec((devices, 1, tok_row, tok_col), lambda c: (0, c, 0, 0)),
+        scratch_shapes=[
+            pltpu.VMEM((length, length), jnp.bfloat16),
+            pltpu.VMEM((length, length), jnp.bfloat16),
+        ],
+        name="triangle_product",
+    )(received)
 
 
 def on_device(
@@ -58,11 +199,12 @@
     alignments = jnp.take(alignment_pool, sample_index, axis=0)
     align_norm = normalize(alignments, 2).astype(jnp.bfloat16)
     align_rows = align_norm.reshape(samples, tok_row * align_width)
-    gathered = lax.all_gather(align_rows, "row", axis=1, tiled=True)
-    column_flat = lax.dynamic_slice_in_dim(
-        gathered, column_start * align_width, tok_col * align_width, 1
-    )
-    column_norm = column_flat.reshape(samples, tok_col, align_width)
+    gathered = gather_blocks(align_rows, 0)
+    column_norm = (
+        gathered.reshape(n_row // n_col, samples, tok_row, align_width)
+        .transpose(1, 0, 2, 3)
+        .reshape(samples, tok_col, align_width)
+    )
     row_factor = jnp.dot(
         align_norm, outer_proj[:, :outer_width], preferred_element_type=jnp.float32
     ).astype(jnp.bfloat16)
@@ -115,10 +257,8 @@
     partial_sum = jnp.einsum(
         "hij,hjk->hik", weights_low, column_values, preferred_element_type=jnp.float32
     )
-    weighted, totals = (
-        lax.psum(partial_sum.astype(jnp.bfloat16), "col").astype(jnp.float32),
-        lax.psum(partial_total.astype(jnp.bfloat16), "col").astype(jnp.float32),
-    )
+    weighted = sum_columns(partial_sum, jnp.bfloat16)
+    totals = sum_columns(partial_total, jnp.float32)
     gate_values = jax.nn.sigmoid(
         jnp.einsum("sim,mhc->hisc", align_norm, gate_weight, preferred_element_type=jnp.float32)
     )
@@ -145,9 +285,7 @@
     group_size = pair_width // (n_row * n_col)
     grouped = factors.reshape(2, n_row * n_col, group_size, tok_row, tok_col)
     received = lax.all_to_all(grouped, ("row", "col"), split_axis=1, concat_axis=1, tiled=True)
-    arranged = received.reshape(2, n_row, n_col, received.shape[2], tok_row, tok_col)
-    result = triangle_product(arranged, n_row, n_col)
-    flat_result = result.reshape(n_row * n_col, result.shape[2], tok_row, tok_col)
+    flat_result = triangle_product(received, n_row, n_col)
     product = lax.all_to_all(flat_result, ("row", "col"), split_axis=0, concat_axis=0, tiled=True)
     product = product.reshape(pair_width, tok_row, tok_col)
     product_norm = normalize(product, 0).astype(jnp.bfloat16).reshape(pair_width, tok_row * tok_col)

time: 165 us -> 119 us (0.72)
  waiting for transfers between devices: 64.8 us -> 19.1 us
  Pallas kernels: 0 us -> 18.7 us
  between operations: 14.5 us -> 1.11 us
  starting transfers between devices: 7.39 us -> 18.1 us
  blocking collectives: 8.55 us -> 0 us
  local copies, waits for them, and re-layouts: 40.2 us -> 33.3 us
    all_gather x1 -> x0, waiting for transfers between devices: 42.9 us -> none  [on_device(): gathered = lax.all_gather(align_rows, 'row', axis=1, tiled=True)]
    pallas_call x0 -> x2, Pallas kernels: none -> 18.7 us  [the longest x1 15 us: gather_blocks(): pl.pallas_call(functools.partial(gather_kernel, n_row, n_col), out_shape=...]
    all_to_all x1, waiting for transfers between devices: 18.1 us -> 1.11 us  [on_device(): lax.all_to_all(grouped, ('row', 'col'), split_axis=1, concat_axis=1, tile...]
    ppermute x0 -> x2, waiting for transfers between devices: none -> 15.2 us  [sum_columns(): total = total + lax.ppermute(sent, 'col', pairs).astype(jnp.float32)]
    convert_element_type x3 -> x0, local copies, waits for them, and re-layouts: 9.76 us -> none  [triangle_product(): return product.transpose(1, 3, 0, 2, 4).astype(jnp.bfloat16)]
    psum x1 -> x0, blocking collectives: 8.55 us -> none  [on_device(): lax.psum(partial_total.astype(jnp.bfloat16), 'col').astype(jnp.float32)]
    all_to_all x1, starting transfers between devices: 3.45 us -> 11.8 us  [on_device(): lax.all_to_all(grouped, ('row', 'col'), split_axis=1, concat_axis=1, tile...]
    psum x1 -> x0, waiting for transfers between devices: 3.71 us -> none  [on_device(): lax.psum(partial_sum.astype(jnp.bfloat16), 'col').astype(jnp.float32)]
  transfers between devices with their start and end apart: 4 -> 4, of which waited for: 3 -> 3; matrix products, arithmetic and copies ran while one was open for 17% -> 18% of each run, Pallas kernels for 0% -> 3%
where the time goes in v1:
time: 119 us; the launch traced here: 118 us
  local copies, waits for them, and re-layouts  33.3 us (28%)
  waiting for transfers between devices  19.1 us (16%)
  Pallas kernels  18.7 us (16%)
  starting transfers between devices  18.1 us (15%)
  matrix products  17.9 us (15%)
  other arithmetic  9.67 us (8%)
    ppermute x2, waiting for transfers between devices, sum_columns(): total = total + lax.ppermute(sent, 'col', pairs).astype(jnp.float32)  15.2 us
    pallas_call x1, Pallas kernels, gather_blocks(): pl.pallas_call(functools.partial(gather_kernel, n_row, n_col), out_shape=...  15 us
    all_to_all x1, starting transfers between devices, on_device(): lax.all_to_all(grouped, ('row', 'col'), split_axis=1, concat_axis=1, tile...  11.8 us
    unnamed x46, local copies, waits for them, and re-layouts  9.5 us
    reshape x2, local copies, waits for them, and re-layouts, on_device(): weighted = weighted.reshape(head_count, tok_row, samples, head_dim)  5.54 us
    all_to_all x1, starting transfers between devices, on_device(): lax.all_to_all(flat_result, ('row', 'col'), split_axis=0, concat_axis=0,...  4.24 us
    pallas_call x1, Pallas kernels, triangle_product(): pl.pallas_call(functools.partial(product_kernel, n_row, n_col, tok_row, t...  3.74 us
    reshape x2, local copies, waits for them, and re-layouts, on_device(): gathered.reshape(n_row // n_col, samples, tok_row, align_width)  3.56 us
  transfers between devices with their start and end apart: 4, of which 3 were waited for; matrix products, arithmetic and copies ran while one was open for 18% of the time, Pallas kernels for 3%

profile of v1, /device:TPU:0, one launch (start us, length us, event | category | flops | bytes accessed | tf_op | source)
XLA Modules:
  0.0 117.9 jit_solution(15099470012297519573)
XLA Ops:
  2.0 2.0 %copy.80 = bf16[256,16,64]{2,1,0:T(8,128)(2,1)S(1)} copy(bf16[256,16,64]{0,2,1:T(8,128)(2,1)} %param.18) | data formatting | bytes 1048576 | tf_op args[1]
  7.3 15.0 %gather_0.1 = bf16[8,64,1024]{2,1,0:T(8,128)(2,1)} custom-call(bf16[64,1024]{1,0:T(8,128)(2,1)} %divide_convert_fusion.block_ref), custom_call_target="tpu_custom_call" | custom-call | tf_op jit(solution)/shard_map/gather_0/pallas_call | solution.py:106
  22.2 3.0 %reshape.284 = bf16[8,64,16,64]{3,2,1,0:T(8,128)(2,1)S(1)} reshape(bf16[8,64,1024]{2,1,0:T(8,128)(2,1)} %gather_0.1) | data formatting | bytes 2097152 | tf_op jit(solution)/shard_map/reshape | solution.py:204
  27.2 0.9 convolution_convert_fusion
  28.2 1.7 %copy.88 = bf16[64,128,32]{0,2,1:T(8,128)(2,1)S(1)} copy(bf16[64,128,32]{1,2,0:T(8,128)(2,1)S(1)} %convolution_convert_fusion) | data formatting | bytes 1048576 | tf_op jit(solution)/shard_map/convert_element_type | solution.py:213
  29.9 7.1 %while.20 = (s32[]{:T(128)}, bf16[2,8,128,128]{3,2,1,0:T(8,128)(2,1)S(1)}, bf16[2,8,128,128]{3,2,1,0:T(8,128)(2,1)S(1)}, bf16[2,64,256]{1,2,0:T(8,128)(2,1)S(1)}...) while((s32[]{:T(128)}, bf16[2,8,128,128]{3,2,1,0:T(8,128)(2,1)S(1)}, ...), condition=%wide.region_3.4_spmd, body=%wide.region_2.3_spmd.sunk | while | flops 405143552 | bytes 10846293 | solution.py:240
  29.9 1.1 copy.143
  33.4 1.1 copy.143
  39.9 1.5 %slice_multiply_fusion.2 = (f32[128,2048]{0,1:T(8,128)S(1)}, f32[128,2048]{0,1:T(8,128)}) fusion(f32[512,2048]{0,1:T(8,128)S(1)} %convolution_bitcast_fusion), kind=kLoop, calls=%fused_computation.58 | loop fusion | flops 2097152 | bytes 6291456 | tf_op jit(solution)/shard_map/mul | solution.py:282
  42.0 2.5 %copy.90 = f32[128,2048]{1,0:T(8,128)} copy(f32[128,2048]{0,1:T(8,128)} %get-tuple-element.94) | data formatting | bytes 2097152 | tf_op jit(solution)/shard_map/mul | solution.py:283
  44.6 1.4 %copy.118 = f32[16,8,16,128]{3,2,1,0:T(8,128)S(1)} copy(f32[16,8,16,128]{3,1,2,0:T(8,128)} %bitcast.215) | data formatting | bytes 2097152
  46.6 1.2 %copy.91 = bf16[2,32,4,16,128]{4,3,2,0,1:T(8,128)(2,1)} copy(bf16[2,32,4,16,128]{4,3,2,1,0:T(8,128)(2,1)S(1)} %pad_maximum_fusion) | data formatting | bytes 2097152 | tf_op jit(solution)/shard_map/stack | solution.py:284
  47.9 11.8 %all-to-all-start = ((bf16[2,32,4,16,128]{4,3,2,0,1:T(8,128)(2,1)}), bf16[2,32,4,16,128]{4,3,2,0,1:T(8,128)(2,1)}, u32[]{:S(2)}, u32[]{:S(2)}) async-start(bf16[2,32,4,16,128]{4,3,2,0,1:T(8,128)(2,1)} %copy.91), calls=%async_computation | async-start | bytes 2097152 | tf_op jit(solution)/shard_map/all_to_all | solution.py:287
  59.8 1.3 %convert_bitcast_fusion.1 = bf16[8,128,64,32]{1,3,0,2:T(8,128)(2,1)S(1)} fusion(bf16[64,128,64,1]{2,1,3,0:T(8,128)(2,1)S(1)} %bitcast.207, bf16[64,8,32,1]{0,2,1,3:T(8,128)(2,1)S(1)} %bitcast.217), kind=kOutput, calls=%fused_computation.31 | convolution fusion | flops 270532608 | bytes 5275648 | tf_op jit(solution)/shard_map/sjm,mhc->hjsc/dot_general | solution.py:251
  61.1 0.9 copy.96
  62.9 1.2 %fusion.79 = (bf16[8,16,2048]{2,1,0:T(8,128)(2,1)S(1)}, f32[8,16,2048]{2,1,0:T(8,128)S(1)}) fusion(bf16[8,128,2048]{1,2,0:T(8,128)(2,1)S(1)} %bitcast.208, bf16[8,16,128]{2,0,1:T(8,128)(2,1)S(1)} %get-tuple-element.98), kind=kOutput, calls=%fused_computation.120 | convolution fusion | flops 67371008 | bytes 5799936 | tf_op jit(solution)/shard_map/hij,hjk->hik/dot_general | solution.py:257
  64.1 1.5 %collective-permute-start = (bf16[8,16,2048]{2,1,0:T(8,128)(2,1)S(1)}, bf16[8,16,2048]{2,1,0:T(8,128)(2,1)S(1)}, u32[]{:S(2)}, u32[]{:S(2)}) collective-permute-start(bf16[8,16,2048]{2,1,0:T(8,128)(2,1)S(1)} %get-tuple-element.109), channel_id=1, source_target_pairs={{0,1},{1,0},{2,3},{3,2},{4,5},{5,4},{6,7},{7,6},{8,9},{9,8},{10,11... | collective-permute-start | bytes 1572872 | tf_op jit(solution)/shard_map/ppermute | solution.py:130
  66.2 2.2 %fusion.26 = f32[2048,128]{1,0:T(8,128)} fusion(bf16[2048,128]{1,0:T(8,128)(2,1)S(1)} %copy-done.5, bf16[128,640]{1,0:T(8,128)(2,1)} %param.26), kind=kOutput, calls=%fused_computation.38 | convolution fusion | flops 67895296 | bytes 1605632 | tf_op jit(solution)/shard_map/dot_general | solution.py:296
  69.2 15.2 %collective-permute-done.1 = f32[8,16]{0,1:T(8,128)S(1)} collective-permute-done((f32[8,16]{0,1:T(8,128)S(1)}, f32[8,16]{0,1:T(8,128)S(1)}, u32[]{:S(2)}, u32[]{:S(2)}) %collective-permute-start.1) | collective-permute-done | bytes 544 | tf_op jit(solution)/shard_map/ppermute | solution.py:130
  84.5 1.1 all-to-all-done
  85.6 2.4 %copy.92.received_ref = bf16[2,32,4,16,128]{4,3,2,1,0:T(8,128)(2,1)} copy(bf16[2,32,4,16,128]{4,3,2,0,1:T(8,128)(2,1)} %all-to-all-done) | data formatting | bytes 2097152 | tf_op jit(solution)/shard_map/all_to_all | solution.py:287
  88.0 3.7 %triangle_product.1 = bf16[32,4,16,128]{3,2,1,0:T(8,128)(2,1)} custom-call(bf16[2,32,4,16,128]{4,3,2,1,0:T(8,128)(2,1)} %copy.92.received_ref), custom_call_target="tpu_custom_call" | custom-call | tf_op jit(solution)/shard_map/triangle_product/pallas_call | solution.py:154
  91.8 4.2 %all-to-all-start.1 = ((bf16[32,4,16,128]{3,2,1,0:T(8,128)(2,1)}), bf16[32,4,16,128]{3,2,1,0:T(8,128)(2,1)S(1)}, u32[]{:S(2)}, u32[]{:S(2)}) async-start(bf16[32,4,16,128]{3,2,1,0:T(8,128)(2,1)} %triangle_product.1), calls=%async_computation.1 | async-start | bytes 1048576 | tf_op jit(solution)/shard_map/all_to_all | solution.py:289
  96.8 1.1 convert_add_fusion
  98.0 2.7 %reshape.292 = f32[8,16,64,32]{3,2,1,0:T(8,128)} reshape(f32[8,16,2048]{2,1,0:T(8,128)S(1)} %convert_add_fusion) | data formatting | bytes 2097152 | tf_op jit(solution)/shard_map/reshape | solution.py:265
  100.7 2.8 %copy.99 = f32[8,16,64,32]{2,3,1,0:T(8,128)S(1)} copy(f32[8,16,64,32]{3,2,1,0:T(8,128)} %reshape.292) | data formatting | bytes 2097152 | tf_op jit(solution)/shard_map/reshape | solution.py:265
  103.5 2.8 %fusion.31 = bf16[64,16,64]{2,0,1:T(8,128)(2,1)} fusion(bf16[8,32,64,1]{2,1,3,0:T(8,128)(2,1)} %bitcast.219, f32[8,16,64,32]{2,3,1,0:T(8,128)S(1)} %copy.99, f32[8,16]{1,0:T(8,128)S(1)} %copy.100, bf16[64,8,32,1]{0,2,3,1:T(8,128)(2,1)S(1)} %bitcast.218, f32[64,16]{0,1:T(8,128)S(1)} %add_sqrt_fusion.2, f32[64,16]{0,1:T(8,128)S(1)} %broadcast_multiply_fusion.4, ...), kind=kOutput, calls=%fused_computation.46 | convolution fusion | flops 69271552 | bytes 1385024 | tf_op jit(solution)/shard_map/hisc,hcm->sim/dot_general | solution.py:267
  106.3 1.9 %copy.102 = bf16[64,16,64]{2,1,0:T(8,128)(2,1)} copy(bf16[64,16,64]{2,0,1:T(8,128)(2,1)} %fusion.31) | data formatting | bytes 262144
  108.3 2.7 %all-to-all-done.1 = bf16[32,4,16,128]{3,2,1,0:T(8,128)(2,1)S(1)} async-done(((bf16[32,4,16,128]{3,2,1,0:T(8,128)(2,1)}), bf16[32,4,16,128]{3,2,1,0:T(8,128)(2,1)S(1)}, u32[]{:S(2)}, u32[]{:S(2)}) %all-to-all-start.1) | async-done | bytes 524320 | tf_op jit(solution)/shard_map/all_to_all | solution.py:289
  112.5 5.5 %while.21 = (s32[]{:T(128)}, bf16[2,1024,128]{2,1,0:T(8,128)(2,1)}, bf16[2,1024,128]{2,1,0:T(8,128)(2,1)S(1)}, bf16[128,1024]{1,0:T(8,128)(2,1)S(1)}, bf16[512,128]{1,0:T(8,128)(2,1)S(1)}, /*index=5*/s32[]{:T(128)}) while((s32[]{:T(128)}, bf16[2,1024,128]{2,1,0:T(8,128)(2,1)}, bf16[2,1024,128]{2,1,0:T(8,128)(2,1)S(1)}, ...), condition=%wide.region_11.12_spmd, body=%wide.region_8.11_spmd.sunk | while | flops 407503872 | bytes 10130001 | solution.py:314
  113.8 1.4 %fusion.119 = bf16[2,1024,128]{2,1,0:T(8,128)(2,1)} fusion(bf16[2,1024,128]{2,1,0:T(8,128)(2,1)} %get-tuple-element.207, s32[]{:T(128)} %get-tuple-element.206, bf16[512,128]{1,0:T(8,128)(2,1)S(1)} %get-tuple-element.216, f32[1024,1024]{1,0:T(8,128)S(1)} %fusion.118, bf16[2,1024,128]{2,1,0:T(8,128)(2,1)S(1)} %get-tuple-element.214), kind=kOutput, calls=%fused_computation.15.clone.1 | convolution fusion | flops 137756672 | bytes 4850176 | tf_op jit(solution)/shard_map/while/body/eval_jaxpr/dot_general | solution.py:311
  116.5 1.4 %fusion.119 = bf16[2,1024,128]{2,1,0:T(8,128)(2,1)} fusion(bf16[2,1024,128]{2,1,0:T(8,128)(2,1)} %get-tuple-element.207, s32[]{:T(128)} %get-tuple-element.206, bf16[512,128]{1,0:T(8,128)(2,1)S(1)} %get-tuple-element.216, f32[1024,1024]{1,0:T(8,128)S(1)} %fusion.118, bf16[2,1024,128]{2,1,0:T(8,128)(2,1)S(1)} %get-tuple-element.214), kind=kOutput, calls=%fused_computation.15.clone.1 | convolution fusion | flops 137756672 | bytes 4850176 | tf_op jit(solution)/shard_map/while/body/eval_jaxpr/dot_general | solution.py:311
  (105 shorter events, 22.8 us)
Async XLA Ops:
  0.6 110.8 %copy-start = (bf16[128,128]{1,0:T(8,128)(2,1)S(1)}, bf16[128,128]{1,0:T(8,128)(2,1)}, u32[]{:S(2)}) copy-start(bf16[128,128]{1,0:T(8,128)(2,1)} %param.27) | copy-start | bytes 98308
  2.0 23.8 %copy-start.11 = (pred[64]{0:T(512)(128)(4,1)}, pred[64]{0:T(512)(128)(4,1)S(1)}, u32[]{:S(2)}) copy-start(pred[64]{0:T(512)(128)(4,1)S(1)} %compare_and_fusion) | copy-start | bytes 196
  25.2 0.7 copy-start.10
  25.9 1.3 %copy-start.1 = (bf16[8,64,16,64]{3,2,0,1:T(8,128)(2,1)}, bf16[8,64,16,64]{3,2,0,1:T(8,128)(2,1)S(1)}, u32[]{:S(2)}) copy-start(bf16[8,64,16,64]{3,2,0,1:T(8,128)(2,1)S(1)} %copy.85) | copy-start | bytes 3145732
  27.2 2.6 %copy-start.14 = (bf16[16,128,128]{2,1,0:T(8,128)(2,1)S(1)}, bf16[16,128,128]{2,1,0:T(8,128)(2,1)}, u32[]{:S(2)}) copy-start(bf16[16,128,128]{2,1,0:T(8,128)(2,1)} %param.17) | copy-start | bytes 1572868
  27.2 2.6 %copy-start.15 = (bf16[1024,128]{1,0:T(8,128)(2,1)S(1)}, bf16[1024,128]{1,0:T(8,128)(2,1)}, u32[]{:S(2)}) copy-start(bf16[1024,128]{1,0:T(8,128)(2,1)} %param.22) | copy-start | bytes 786436
  36.9 2.3 %copy-start.7 = (bf16[128,640]{1,0:T(8,128)(2,1)S(1)}, bf16[128,640]{1,0:T(8,128)(2,1)}, u32[]{:S(2)}) copy-start(bf16[128,640]{1,0:T(8,128)(2,1)} %param.26) | copy-start | bytes 491524
  38.5 0.8 copy-start.4
  42.0 4.0 %copy-start.17 = (s32[256]{0:T(256)S(1)}, s32[256]{0:T(256)}, u32[]{:S(2)}) copy-start(s32[256]{0:T(256)} %param.20) | copy-start | bytes 3076
  46.6 13.0 %copy-start.8 = (bf16[64,512]{1,0:T(8,128)(2,1)S(1)}, bf16[64,512]{1,0:T(8,128)(2,1)}, u32[]{:S(2)}) copy-start(bf16[64,512]{1,0:T(8,128)(2,1)} %param.24) | copy-start | bytes 196612
  46.6 13.2 %copy-start.2 = (bf16[8,64,16,64]{3,2,0,1:T(8,128)(2,1)S(1)}, bf16[8,64,16,64]{3,2,0,1:T(8,128)(2,1)}, u32[]{:S(2)}) copy-start(bf16[8,64,16,64]{3,2,0,1:T(8,128)(2,1)} %copy-done.1) | copy-start | bytes 3145732
  47.9 37.7 %all-to-all-start = ((bf16[2,32,4,16,128]{4,3,2,0,1:T(8,128)(2,1)}), bf16[2,32,4,16,128]{4,3,2,0,1:T(8,128)(2,1)}, u32[]{:S(2)}, u32[]{:S(2)}) async-start(bf16[2,32,4,16,128]{4,3,2,0,1:T(8,128)(2,1)} %copy.91), calls=%async_computation | async-start | bytes 2097152 | tf_op jit(solution)/shard_map/all_to_all | solution.py:287
  61.1 1.5 %copy-start.13 = (bf16[128,8]{0,1:T(8,128)(2,1)S(1)}, bf16[128,8]{0,1:T(8,128)(2,1)}, u32[]{:S(2)}) copy-start(bf16[128,8]{0,1:T(8,128)(2,1)} %param.23) | copy-start | bytes 6148
  62.9 3.3 %copy-start.5 = (bf16[2048,128]{1,0:T(8,128)(2,1)S(1)}, bf16[2048,128]{1,0:T(8,128)(2,1)}, u32[]{:S(2)}) copy-start(bf16[2048,128]{1,0:T(8,128)(2,1)} %copy-done.4) | copy-start | bytes 1572868
  64.1 31.9 %collective-permute-start = (bf16[8,16,2048]{2,1,0:T(8,128)(2,1)S(1)}, bf16[8,16,2048]{2,1,0:T(8,128)(2,1)S(1)}, u32[]{:S(2)}, u32[]{:S(2)}) collective-permute-start(bf16[8,16,2048]{2,1,0:T(8,128)(2,1)S(1)} %get-tuple-element.109), channel_id=1, source_target_pairs={{0,1},{1,0},{2,3},{3,2},{4,5},{5,4},{6,7},{7,6},{8,9},{9,8},{10,11... | collective-permute-start | bytes 1572872 | tf_op jit(solution)/shard_map/ppermute | solution.py:130
  65.6 2.8 %copy-start.9 = (bf16[256,64]{0,1:T(8,128)(2,1)S(1)}, bf16[256,64]{0,1:T(8,128)(2,1)}, u32[]{:S(2)}) copy-start(bf16[256,64]{0,1:T(8,128)(2,1)} %param.25) | copy-start | bytes 98308
  65.6 18.8 %collective-permute-start.1 = (f32[8,16]{0,1:T(8,128)S(1)}, f32[8,16]{0,1:T(8,128)S(1)}, u32[]{:S(2)}, u32[]{:S(2)}) collective-permute-start(f32[8,16]{0,1:T(8,128)S(1)} %get-tuple-element.97), channel_id=1, source_target_pairs={{0,1},{1,0},{2,3},{3,2},{4,5},{5,4},{6,7},{7,6},{8,9},{9,8},{10,11... | collective-permute-start | bytes 1544 | tf_op jit(solution)/shard_map/ppermute | solution.py:130
  91.8 19.2 %all-to-all-start.1 = ((bf16[32,4,16,128]{3,2,1,0:T(8,128)(2,1)}), bf16[32,4,16,128]{3,2,1,0:T(8,128)(2,1)S(1)}, u32[]{:S(2)}, u32[]{:S(2)}) async-start(bf16[32,4,16,128]{3,2,1,0:T(8,128)(2,1)} %triangle_product.1), calls=%async_computation.1 | async-start | bytes 1048576 | tf_op jit(solution)/shard_map/all_to_all | solution.py:289
  96.0 0.8 copy-start.6
  100.7 2.8 %copy-start.12 = (pred[64]{0:T(512)(128)(4,1)S(1)}, pred[64]{0:T(512)(128)(4,1)}, u32[]{:S(2)}) copy-start(pred[64]{0:T(512)(128)(4,1)} %copy-done.11) | copy-start | bytes 196
  106.3 5.1 %copy-start.18 = (f32[2048,128]{1,0:T(8,128)S(1)}, f32[2048,128]{1,0:T(8,128)}, u32[]{:S(2)}) copy-start(f32[2048,128]{1,0:T(8,128)} %fusion.26) | copy-start | bytes 3145732
  111.5 1.0 copy-start.3
  111.5 1.0 copy-start.16

commit v2 on v1

--- a/solution.py
+++ b/solution.py
@@ -136,8 +136,8 @@
         for u in range(n_col):
             rows = slice(r * tok_row, (r + 1) * tok_row)
             lanes = slice(u * tok_col, (u + 1) * tok_col)
-            left_ref[rows, lanes] = received_ref[0, r * n_col + u, 0]
-            right_ref[rows, lanes] = received_ref[1, r * n_col + u, 0]
+            left_ref[rows, lanes] = received_ref[r * n_col + u, 0, 0]
+            right_ref[rows, lanes] = received_ref[r * n_col + u, 1, 0]
     result = lax.dot_general(
         left_ref[...], right_ref[...], (((1,), (1,)), ((), ())), preferred_element_type=jnp.float32
     ).astype(jnp.bfloat16)
@@ -149,14 +149,14 @@
 
 
 def triangle_product(received, n_row, n_col):
-    _, devices, items, tok_row, tok_col = received.shape
+    devices, _, items, tok_row, tok_col = received.shape
     length = n_row * tok_row
     return pl.pallas_call(
         functools.partial(product_kernel, n_row, n_col, tok_row, tok_col),
         grid=(items,),
         out_shape=jax.ShapeDtypeStruct((devices, items, tok_row, tok_col), jnp.bfloat16),
         in_specs=[
-            pl.BlockSpec((2, devices, 1, tok_row, tok_col), lambda c: (0, 0, c, 0, 0))
+            pl.BlockSpec((devices, 2, 1, tok_row, tok_col), lambda c: (0, 0, c, 0, 0))
         ],
         out_specs=pl.BlockSpec((devices, 1, tok_row, tok_col), lambda c: (0, c, 0, 0)),
         scratch_shapes=[
@@ -165,6 +165,227 @@
         ],
         name="triangle_product",
     )(received)
+
+
+def prep_kernel(
+    index_ref, pool_ref, row_weight_ref, column_weight_ref, align_ref, norm_ref, row_ref, column_ref, held_ref
+):
+    tok_row, align_width, stored = pool_ref.shape
+    samples = align_ref.shape[1]
+    outer_width = row_weight_ref.shape[1]
+    half = outer_width // 2
+    slots = lax.broadcasted_iota(jnp.int32, (2 * samples, stored), 1)
+    picks = (slots == index_ref[...]).astype(jnp.bfloat16)
+    lanes = lax.broadcasted_iota(jnp.int32, (half, 2 * samples), 1)
+    for t in range(tok_row):
+        twice = lax.dot_general(
+            picks, pool_ref[t], (((1,), (1,)), ((), ())), preferred_element_type=jnp.float32
+        )
+        normed = normalize(twice, 1).astype(jnp.bfloat16)
+        align_ref[t] = twice[:samples].astype(jnp.bfloat16)
+        norm_ref[t] = normed[:samples]
+        row_ref[t * samples : (t + 1) * samples, :] = jnp.dot(
+            normed[:samples], row_weight_ref[...], preferred_element_type=jnp.float32
+        ).astype(jnp.bfloat16)
+        factor = lax.dot_general(
+            column_weight_ref[...],
+            normed,
+            (((1,), (1,)), ((), ())),
+            preferred_element_type=jnp.float32,
+        )
+        held_ref[t * half : (t + 1) * half, :] = jnp.where(
+            lanes < samples, factor[:half], factor[half:]
+        )
+    for d in range(half):
+        column_ref[:, d * 2 * samples : (d + 1) * 2 * samples] = held_ref[
+            pl.ds(d, tok_row, stride=half), :
+        ].astype(jnp.bfloat16)
+
+
+def prepare(alignment_pool, sample_index, outer_proj):
+    stored, tok_row, align_width = alignment_pool.shape
+    samples = sample_index.shape[0]
+    outer_width = outer_proj.shape[1] // 2
+    half = outer_width // 2
+    spread = jnp.concatenate([sample_index, sample_index])[:, None]
+    return pl.pallas_call(
+        prep_kernel,
+        out_shape=(
+            jax.ShapeDtypeStruct((tok_row, samples, align_width), jnp.bfloat16),
+            jax.ShapeDtypeStruct((tok_row, samples, align_width), jnp.bfloat16),
+            jax.ShapeDtypeStruct((tok_row * samples, outer_width), jnp.bfloat16),
+            jax.ShapeDtypeStruct((tok_row, outer_width * samples), jnp.bfloat16),
+        ),
+        scratch_shapes=[pltpu.VMEM((tok_row * half, 2 * samples), jnp.float32)],
+        name="prepare",
+    )(
+        spread,
+        alignment_pool.transpose(1, 2, 0),
+        outer_proj[:, :outer_width],
+        outer_proj[:, outer_width:].T,
+    )
+
+
+def pair_kernel(
+    steps,
+    step_rows,
+    samples,
+    head_count,
+    column_ref,
+    row_ref,
+    mix_ref,
+    grid_ref,
+    weight_ref,
+    mask_ref,
+    one_ref,
+    norm_ref,
+    score_ref,
+    factor_ref,
+    held_ref,
+):
+    step = pl.program_id(0)
+    pair_width = grid_ref.shape[2]
+    outer_width = row_ref.shape[1]
+    half = outer_width // 2
+    tok_row = steps * step_rows
+    order = [side * half + d for d in range(half) for side in range(2)]
+    spread = jnp.dot(row_ref[...], mix_ref[...], preferred_element_type=jnp.float32).astype(
+        jnp.bfloat16
+    )
+    for k in range(step_rows):
+        piece = spread[k * samples : (k + 1) * samples]
+        stacked = jnp.concatenate(
+            [piece[:, d * pair_width : (d + 1) * pair_width] for d in order], axis=0
+        )
+        update = jnp.dot(column_ref[...], stacked, preferred_element_type=jnp.float32)
+        pair_one = (grid_ref[k].astype(jnp.float32) + update * (1.0 / samples)).astype(jnp.bfloat16)
+        one_ref[k] = pair_one
+        pair_norm = normalize(pair_one, 1).astype(jnp.bfloat16)
+        norm_ref[k] = pair_norm
+        projected = lax.dot_general(
+            weight_ref[...],
+            pair_norm,
+            (((1,), (1,)), ((), ())),
+            preferred_element_type=jnp.float32,
+        )
+        mask = mask_ref[k]
+        row = step * step_rows + k
+        for side in range(2):
+            base = 2 * side * pair_width
+            gate = projected[base : base + pair_width]
+            value = projected[base + pair_width : base + 2 * pair_width]
+            held_ref[side, pl.ds(row, pair_width, stride=tok_row), :] = (
+                jax.nn.sigmoid(gate) * value * mask
+            )
+        score_ref[k] = jnp.exp(projected[4 * pair_width : 4 * pair_width + head_count])
+
+    @pl.when(step == steps - 1)
+    def _():
+        devices, _, group, _, tok_col = factor_ref.shape
+        for side in range(2):
+            factor_ref[:, side] = (
+                held_ref[side].astype(jnp.bfloat16).reshape(devices, group, tok_row, tok_col)
+            )
+
+
+def pair_stage(columns, rows, outer_mix, pair_grid, triangle_proj, pair_logit, pair_mask, devices):
+    tok_row, tok_col, pair_width = pair_grid.shape
+    outer_width = rows.shape[1]
+    samples = rows.shape[0] // tok_row
+    head_count = pair_logit.shape[1]
+    step_rows = 2 if tok_row % 2 == 0 else 1
+    steps = tok_row // step_rows
+    group = pair_width // devices
+    mix = outer_mix.reshape(outer_width, outer_width * pair_width)
+    weights = jnp.concatenate([triangle_proj[:, : 4 * pair_width], pair_logit], axis=1).T
+    whole = lambda *shape: pl.BlockSpec(shape, lambda r: (0,) * len(shape))
+    part = lambda *shape: pl.BlockSpec(shape, lambda r: (r,) + (0,) * (len(shape) - 1))
+    return pl.pallas_call(
+        functools.partial(pair_kernel, steps, step_rows, samples, head_count),
+        grid=(steps,),
+        out_shape=(
+            jax.ShapeDtypeStruct(pair_grid.shape, jnp.bfloat16),
+            jax.ShapeDtypeStruct(pair_grid.shape, jnp.bfloat16),
+            jax.ShapeDtypeStruct((tok_row, head_count, tok_col), jnp.float32),
+            jax.ShapeDtypeStruct((devices, 2, group, tok_row, tok_col), jnp.bfloat16),
+        ),
+        in_specs=[
+            whole(*columns.shape),
+            part(step_rows * samples, outer_width),
+            whole(*mix.shape),
+            part(step_rows, tok_col, pair_width),
+            whole(*weights.shape),
+            part(step_rows, 1, tok_col),
+        ],
+        out_specs=(
+            part(step_rows, tok_col, pair_width),
+            part(step_rows, tok_col, pair_width),
+            part(step_rows, head_count, tok_col),
+            whole(devices, 2, group, tok_row, tok_col),
+        ),
+        scratch_shapes=[pltpu.VMEM((2, pair_width * tok_row, tok_col), jnp.float32)],
+        name="pair_stage",
+    )(columns, rows, mix, pair_grid, weights, pair_mask[:, None, :])
+
+
+def tail_kernel(
+    step_rows, product_ref, one_ref, gate_ref, mix_ref, up_ref, down_ref, out_ref, held_ref
+):
+    step = pl.program_id(0)
+    devices, group, tok_row, tok_col = product_ref.shape
+    pair_width = devices * group
+    inner_width = down_ref.shape[0]
+
+    @pl.when(step == 0)
+    def _():
+        held_ref[...] = (
+            product_ref[...].astype(jnp.float32).reshape(pair_width * tok_row, tok_col)
+        )
+
+    rows = []
+    for k in range(step_rows):
+        product = held_ref[pl.ds(step * step_rows + k, pair_width, stride=tok_row), :]
+        normed = normalize(product, 0).astype(jnp.bfloat16)
+        mixed = lax.dot_general(
+            normed, mix_ref[...], (((0,), (0,)), ((), ())), preferred_element_type=jnp.float32
+        )
+        rows.append((one_ref[k].astype(jnp.float32) + gate_ref[k] * mixed).astype(jnp.bfloat16))
+    pair_two = jnp.concatenate(rows, axis=0)
+    normed = normalize(pair_two, 1).astype(jnp.bfloat16)
+    expanded = jnp.dot(normed, up_ref[...], preferred_element_type=jnp.float32)
+    hidden = (jax.nn.silu(expanded[:, :inner_width]) * expanded[:, inner_width:]).astype(
+        jnp.bfloat16
+    )
+    result = (
+        pair_two.astype(jnp.float32)
+        + jnp.dot(hidden, down_ref[...], preferred_element_type=jnp.float32)
+    ).astype(jnp.bfloat16)
+    for k in range(step_rows):
+        out_ref[k] = result[k * tok_col : (k + 1) * tok_col]
+
+
+def tail_stage(product, pair_one, gate_out, triangle_mix, transition_up, transition_down):
+    tok_row, tok_col, pair_width = pair_one.shape
+    step_rows = 2 if tok_row % 2 == 0 else 1
+    whole = lambda *shape: pl.BlockSpec(shape, lambda r: (0,) * len(shape))
+    part = lambda *shape: pl.BlockSpec(shape, lambda r: (r,) + (0,) * (len(shape) - 1))
+    block = part(step_rows, tok_col, pair_width)
+    return pl.pallas_call(
+        functools.partial(tail_kernel, step_rows),
+        grid=(tok_row // step_rows,),
+        out_shape=jax.ShapeDtypeStruct(pair_one.shape, jnp.bfloat16),
+        in_specs=[
+            whole(*product.shape),
+            block,
+            block,
+            whole(*triangle_mix.shape),
+            whole(*transition_up.shape),
+            whole(*transition_down.shape),
+        ],
+        out_specs=block,
+        scratch_shapes=[pltpu.VMEM((pair_width * tok_row, tok_col), jnp.float32)],
+        name="tail_stage",
+    )(product, pair_one, gate_out, triangle_mix, transition_up, transition_down)
 
 
 def on_device(
@@ -189,63 +410,39 @@
     pair_width = pair_grid.shape[2]
     samples = sample_index.shape[0]
     align_width = alignment_pool.shape[2]
-    outer_width = outer_proj.shape[1] // 2
     head_count = pair_logit.shape[1]
     head_total = average_proj.shape[1] // 2
     head_dim = head_total // head_count
-    inner_width = transition_down.shape[0]
     row_start = lax.axis_index("row") * tok_row
     column_start = lax.axis_index("col") * tok_col
-    alignments = jnp.take(alignment_pool, sample_index, axis=0)
-    align_norm = normalize(alignments, 2).astype(jnp.bfloat16)
-    align_rows = align_norm.reshape(samples, tok_row * align_width)
-    gathered = gather_blocks(align_rows, 0)
+    row_mask = lax.dynamic_slice_in_dim(token_mask, row_start, tok_row, 0).astype(jnp.float32)
+    column_mask = lax.dynamic_slice_in_dim(token_mask, column_start, tok_col, 0).astype(jnp.float32)
+    pair_mask = row_mask[:, None] * column_mask[None, :]
+    alignments, align_norm, rows, column_block = prepare(alignment_pool, sample_index, outer_proj)
+    columns = gather_blocks(column_block, 0).reshape(tok_col, column_block.shape[1])
+    pair_one, pair_norm, weights, factors = pair_stage(
+        columns,
+        rows,
+        outer_mix,
+        pair_grid,
+        triangle_proj,
+        pair_logit,
+        pair_mask,
+        n_row * n_col,
+    )
+    received = lax.all_to_all(factors, ("row", "col"), split_axis=0, concat_axis=0, tiled=True)
+    align_rows = align_norm.transpose(1, 0, 2).reshape(samples, tok_row * align_width)
+    align_rows, weights = lax.optimization_barrier((align_rows, weights))
+    gathered = gather_blocks(align_rows, 1)
     column_norm = (
         gathered.reshape(n_row // n_col, samples, tok_row, align_width)
         .transpose(1, 0, 2, 3)
         .reshape(samples, tok_col, align_width)
     )
-    row_factor = jnp.dot(
-        align_norm, outer_proj[:, :outer_width], preferred_element_type=jnp.float32
-    ).astype(jnp.bfloat16)
-    column_factor = jnp.dot(
-        column_norm, outer_proj[:, outer_width:], preferred_element_type=jnp.float32
-    ).astype(jnp.bfloat16)
-    column_rows = column_factor.reshape(samples, tok_col * outer_width)
-    block_rows = 8
-    block_count = tok_row // block_rows
-    row_blocks = row_factor.reshape(samples, block_count, block_rows * outer_width).transpose(
-        1, 0, 2
-    )
-    pair_blocks = pair_grid.reshape(block_count, block_rows, tok_col, pair_width)
-
-    def outer_step(operands):
-        left_block, pair_block = operands
-        outer_sum = lax.dot_general(
-            left_block, column_rows, (((0,), (0,)), ((), ())), preferred_element_type=jnp.float32
-        )
-        outer_sum = outer_sum.reshape(block_rows, outer_width, tok_col, outer_width).transpose(
-            0, 2, 1, 3
-        )
-        outer_mean = (
-            (outer_sum * (1.0 / samples))
-            .astype(jnp.bfloat16)
-            .reshape(block_rows * tok_col, outer_width * outer_width)
-        )
-        update = jnp.dot(outer_mean, outer_mix, preferred_element_type=jnp.float32).reshape(
-            block_rows, tok_col, pair_width
-        )
-        return (pair_block.astype(jnp.float32) + update).astype(jnp.bfloat16)
-
-    pair_one = lax.map(outer_step, (row_blocks, pair_blocks)).reshape(tok_row, tok_col, pair_width)
-    pair_norm = normalize(pair_one, 2).astype(jnp.bfloat16)
     value_weight = average_proj[:, :head_total].reshape(align_width, head_count, head_dim)
     gate_weight = average_proj[:, head_total:].reshape(align_width, head_count, head_dim)
     mix_weight = average_mix.reshape(head_count, head_dim, align_width)
-    scores = lax.dot_general(
-        pair_logit, pair_norm, (((0,), (2,)), ((), ())), preferred_element_type=jnp.float32
-    )
-    weights = jnp.exp(scores)
+    weights = weights.transpose(1, 0, 2)
     partial_total = jnp.sum(weights, axis=2)
     weights_low = weights.astype(jnp.bfloat16)
     column_values = jnp.einsum(
@@ -260,58 +457,24 @@
     weighted = sum_columns(partial_sum, jnp.bfloat16)
     totals = sum_columns(partial_total, jnp.float32)
     gate_values = jax.nn.sigmoid(
-        jnp.einsum("sim,mhc->hisc", align_norm, gate_weight, preferred_element_type=jnp.float32)
+        jnp.einsum("ism,mhc->hisc", align_norm, gate_weight, preferred_element_type=jnp.float32)
     )
     weighted = weighted.reshape(head_count, tok_row, samples, head_dim)
     averaged = (gate_values * weighted / totals[:, :, None, None]).astype(jnp.bfloat16)
     align_update = jnp.einsum(
         "hisc,hcm->sim", averaged, mix_weight, preferred_element_type=jnp.float32
     )
-    alignment_next = (alignments.astype(jnp.float32) + align_update).astype(jnp.bfloat16)
-    flat_norm = pair_norm.reshape(tok_row * tok_col, pair_width)
-    projected = lax.dot_general(
-        triangle_proj[:, : 4 * pair_width],
-        flat_norm,
-        (((0,), (1,)), ((), ())),
-        preferred_element_type=jnp.float32,
-    )
-    projected = projected.reshape(4, pair_width, tok_row, tok_col)
-    row_mask = lax.dynamic_slice_in_dim(token_mask, row_start, tok_row, 0).astype(jnp.float32)
-    column_mask = lax.dynamic_slice_in_dim(token_mask, column_start, tok_col, 0).astype(jnp.float32)
-    pair_mask = row_mask[:, None] * column_mask[None, :]
-    left_side = jax.nn.sigmoid(projected[0]) * projected[1] * pair_mask
-    right_side = jax.nn.sigmoid(projected[2]) * projected[3] * pair_mask
-    factors = jnp.stack([left_side, right_side]).astype(jnp.bfloat16)
-    group_size = pair_width // (n_row * n_col)
-    grouped = factors.reshape(2, n_row * n_col, group_size, tok_row, tok_col)
-    received = lax.all_to_all(grouped, ("row", "col"), split_axis=1, concat_axis=1, tiled=True)
+    alignment_next = (
+        alignments.transpose(1, 0, 2).astype(jnp.float32) + align_update
+    ).astype(jnp.bfloat16)
     flat_result = triangle_product(received, n_row, n_col)
     product = lax.all_to_all(flat_result, ("row", "col"), split_axis=0, concat_axis=0, tiled=True)
-    product = product.reshape(pair_width, tok_row, tok_col)
-    product_norm = normalize(product, 0).astype(jnp.bfloat16).reshape(pair_width, tok_row * tok_col)
-    mixed = lax.dot_general(
-        product_norm, triangle_mix, (((0,), (0,)), ((), ())), preferred_element_type=jnp.float32
-    )
     gate_out = jax.nn.sigmoid(
-        jnp.dot(flat_norm, triangle_proj[:, 4 * pair_width :], preferred_element_type=jnp.float32)
-    )
-    pair_two = (
-        pair_one.reshape(tok_row * tok_col, pair_width).astype(jnp.float32) + gate_out * mixed
-    ).astype(jnp.bfloat16)
-    tail_rows = pair_two.reshape(block_count, block_rows * tok_col, pair_width)
-
-    def transition_step(rows_block):
-        normed = normalize(rows_block, 1).astype(jnp.bfloat16)
-        expanded = jnp.dot(normed, transition_up, preferred_element_type=jnp.float32)
-        hidden = (jax.nn.silu(expanded[:, :inner_width]) * expanded[:, inner_width:]).astype(
-            jnp.bfloat16
-        )
-        return (
-            rows_block.astype(jnp.float32)
-            + jnp.dot(hidden, transition_down, preferred_element_type=jnp.float32)
-        ).astype(jnp.bfloat16)
-
-    pair_next = lax.map(transition_step, tail_rows).reshape(tok_row, tok_col, pair_width)
+        jnp.dot(pair_norm, triangle_proj[:, 4 * pair_width :], preferred_element_type=jnp.float32)
+    )
+    pair_next = tail_stage(
+        product, pair_one, gate_out, triangle_mix, transition_up, transition_down
+    )
     return (pair_next, alignment_next)
 
 

time: 119 us -> 150 us (1.26)
  Pallas kernels: 18.7 us -> 72.4 us
  matrix products: 17.9 us -> 6.73 us
  local copies, waits for them, and re-layouts: 33.3 us -> 22.2 us
  starting transfers between devices: 18.1 us -> 27 us
  other arithmetic: 9.67 us -> 2.51 us
  waiting for transfers between devices: 19.1 us -> 16.5 us
    pallas_call x0 -> x3, Pallas kernels: none -> 30.5 us  [the longest x1 14.5 us: pair_stage(): pl.pallas_call(functools.partial(pair_kernel, steps, step_rows, samples,...]
    pallas_call x1 -> x2, Pallas kernels: 15 us -> 38.2 us  [gather_blocks(): pl.pallas_call(functools.partial(gather_kernel, n_row, n_col), out_shape=...]
    ppermute x2, starting transfers between devices: 2.06 us -> 13.4 us  [sum_columns(): total = total + lax.ppermute(sent, 'col', pairs).astype(jnp.float32)]
    dot_general x14 -> x1, matrix products: 12.6 us -> 1.41 us  [on_device(): jnp.dot(pair_norm, triangle_proj[:, 4 * pair_width:], preferred_element_t...]
    unnamed x46 -> x27, local copies, waits for them, and re-layouts: 9.5 us -> 4.35 us
    ppermute x2, waiting for transfers between devices: 15.2 us -> 10.4 us  [sum_columns(): total = total + lax.ppermute(sent, 'col', pairs).astype(jnp.float32)]
    all_to_all x1, starting transfers between devices: 11.8 us -> 7.88 us  [on_device(): lax.all_to_all(factors, ('row', 'col'), split_axis=0, concat_axis=0, tile...]
    all_to_all x1, waiting for transfers between devices: 2.72 us -> 6.14 us  [on_device(): lax.all_to_all(flat_result, ('row', 'col'), split_axis=0, concat_axis=0,...]
  transfers between devices with their start and end apart: 4 -> 4, of which waited for: 3 -> 2; matrix products, arithmetic and copies ran while one was open for 18% -> 15% of each run, Pallas kernels for 3% -> 20%
where the time goes in v2:
time: 150 us; the launch traced here: 148 us
  Pallas kernels  72.4 us (48%)
  starting transfers between devices  27 us (18%)
  local copies, waits for them, and re-layouts  22.2 us (15%)
  waiting for transfers between devices  16.5 us (11%)
  matrix products  6.73 us (4%)
  other arithmetic  2.51 us (2%)
    pallas_call x2, Pallas kernels, gather_blocks(): pl.pallas_call(functools.partial(gather_kernel, n_row, n_col), out_shape=...  38.2 us
    pallas_call x1, Pallas kernels, pair_stage(): pl.pallas_call(functools.partial(pair_kernel, steps, step_rows, samples,...  14.5 us
    ppermute x2, starting transfers between devices, sum_columns(): total = total + lax.ppermute(sent, 'col', pairs).astype(jnp.float32)  13.4 us
    ppermute x2, waiting for transfers between devices, sum_columns(): total = total + lax.ppermute(sent, 'col', pairs).astype(jnp.float32)  10.4 us
    pallas_call x1, Pallas kernels, tail_stage(): pl.pallas_call(functools.partial(tail_kernel, step_rows), grid=(tok_row /...  9.36 us
    all_to_all x1, starting transfers between devices, on_device(): lax.all_to_all(factors, ('row', 'col'), split_axis=0, concat_axis=0, tile...  7.88 us
    pallas_call x1, Pallas kernels, prepare(): pl.pallas_call(prep_kernel, out_shape=(jax.ShapeDtypeStruct((tok_row, sam...  6.68 us
    reshape x2, local copies, waits for them, and re-layouts, on_device(): gathered.reshape(n_row // n_col, samples, tok_row, align_width)  6.27 us
  transfers between devices with their start and end apart: 4, of which 2 were waited for; matrix products, arithmetic and copies ran while one was open for 15% of the time, Pallas kernels for 20%

profile of v2, /device:TPU:0, one launch (start us, length us, event | category | flops | bytes accessed | tf_op | source)
XLA Modules:
  0.0 148.3 jit_solution(11548368252637918550)
XLA Ops:
  0.7 0.8 add_bitcast_fusion
  1.5 0.7 copy.40.index_ref
  2.2 1.4 fusion.19
  3.6 0.7 copy.60
  4.3 6.7 %prepare.1 = (bf16[16,64,64]{2,1,0:T(8,128)(2,1)}, bf16[16,64,64]{2,1,0:T(8,128)(2,1)}, bf16[1024,32]{1,0:T(8,128)(2,1)}, bf16[16,2048]{1,0:T(8,128)(2,1)}) custom-call(s32[128,1]{1,0:T(8,128)} %copy.40.index_ref, bf16[16,64,256]{2,1,0:T(8,128)(2,1)} %bitcast.67, bf16[64,32]{1,0:T(8,128)(2,1)} %get-tuple-element.31.row_weight_ref, bf16[32,64]{1,0:T(8,128)(2,1)} %bitcast.72), custom_call_target="tpu_custom_call" | custom-call | tf_op jit(solution)/shard_map/prepare/pallas_call | solution.py:211
  11.0 12.0 %gather_0.1 = bf16[8,16,2048]{2,1,0:T(8,128)(2,1)} custom-call(bf16[16,2048]{1,0:T(8,128)(2,1)} %get-tuple-element.12.block_ref), custom_call_target="tpu_custom_call" | custom-call | tf_op jit(solution)/shard_map/gather_0/pallas_call | solution.py:106
  23.0 1.8 %reshape.75.mix_ref = bf16[32,4096]{1,0:T(8,128)(2,1)} reshape(bf16[1024,128]{1,0:T(8,128)(2,1)} %param.18) | data formatting | bytes 524288 | tf_op jit(solution)/shard_map/reshape | solution.py:299
  25.1 0.7 maximum_bitcast_fusion.weight_ref
  25.8 0.7 broadcast_multiply_fusion.mask_ref
  26.4 14.5 %pair_stage.1 = (bf16[16,128,128]{2,1,0:T(8,128)(2,1)}, bf16[16,128,128]{2,1,0:T(8,128)(2,1)}, f32[16,8,128]{2,1,0:T(8,128)}, bf16[32,2,4,16,128]{4,3,2,1,0:T(8,128)(2,1)}) custom-call(bf16[128,2048]{1,0:T(8,128)(2,1)} %bitcast.66, bf16[1024,32]{1,0:T(8,128)(2,1)} %get-tuple-element.13.row_ref, bf16[32,4096]{1,0:T(8,128)(2,1)} %reshape.75.mix_ref, ...), custom_call_target="tpu_custom_call" | custom-call | tf_op jit(solution)/shard_map/pair_stage/pallas_call | solution.py:303
  40.9 7.9 %all-to-all-start = ((bf16[32,2,4,16,128]{4,3,2,1,0:T(8,128)(2,1)}), bf16[32,2,4,16,128]{4,3,2,1,0:T(8,128)(2,1)S(1)}, u32[]{:S(2)}, u32[]{:S(2)}) async-start(bf16[32,2,4,16,128]{4,3,2,1,0:T(8,128)(2,1)} %get-tuple-element.14), calls=%async_computation | async-start | bytes 2097152 | tf_op jit(solution)/shard_map/all_to_all | solution.py:433
  49.0 0.9 reshape.77.block_ref
  49.8 26.2 %gather_1.1 = bf16[8,64,1024]{2,1,0:T(8,128)(2,1)} custom-call(bf16[64,1024]{1,0:T(8,128)(2,1)} %reshape.77.block_ref), custom_call_target="tpu_custom_call" | custom-call | tf_op jit(solution)/shard_map/gather_1/pallas_call | solution.py:106
  76.0 4.0 %reshape.78 = bf16[8,64,16,64]{3,2,1,0:T(8,128)(2,1)} reshape(bf16[8,64,1024]{2,1,0:T(8,128)(2,1)} %gather_1.1) | data formatting | bytes 2097152 | tf_op jit(solution)/shard_map/reshape | solution.py:438
  80.1 2.2 %copy.44 = bf16[8,64,16,64]{3,2,0,1:T(8,128)(2,1)S(1)} copy(bf16[8,64,16,64]{3,2,1,0:T(8,128)(2,1)} %reshape.78) | data formatting | bytes 2097152 | tf_op jit(solution)/shard_map/reshape | solution.py:438
  82.5 1.3 convert_bitcast_fusion
  83.7 0.9 copy.47
  84.7 2.0 %fusion.20 = (bf16[8,16,2048]{2,1,0:T(8,128)(2,1)}, f32[8,16,2048]{2,1,0:T(8,128)S(1)}) fusion(bf16[8,128,2048]{1,2,0:T(8,128)(2,1)S(1)} %bitcast.64, bf16[8,16,128]{2,0,1:T(8,128)(2,1)S(1)} %bitcast_convert_fusion), kind=kOutput, calls=%fused_computation.29 | convolution fusion | flops 67371008 | bytes 5799936 | tf_op jit(solution)/shard_map/hij,hjk->hik/dot_general | solution.py:454
  86.7 13.3 %collective-permute-start = (bf16[8,16,2048]{2,1,0:T(8,128)(2,1)}, bf16[8,16,2048]{2,1,0:T(8,128)(2,1)S(1)}, u32[]{:S(2)}, u32[]{:S(2)}) collective-permute-start(bf16[8,16,2048]{2,1,0:T(8,128)(2,1)} %get-tuple-element.32), channel_id=1, source_target_pairs={{0,1},{1,0},{2,3},{3,2},{4,5},{5,4},{6,7},{7,6},{8,9},{9,8},{10,11... | collective-permute-start | bytes 1572872 | tf_op jit(solution)/shard_map/ppermute | solution.py:130
  100.2 1.4 fusion.4.gate_ref
  101.7 0.7 copy.62
  102.5 10.4 %collective-permute-done.1 = f32[8,16]{0,1:T(8,128)S(1)} collective-permute-done((f32[8,16]{0,1:T(8,128)S(1)}, f32[8,16]{0,1:T(8,128)S(1)}, u32[]{:S(2)}, u32[]{:S(2)}) %collective-permute-start.1) | collective-permute-done | bytes 544 | tf_op jit(solution)/shard_map/ppermute | solution.py:130
  112.9 1.0 copy-done
  113.9 3.7 %triangle_product.1 = bf16[32,4,16,128]{3,2,1,0:T(8,128)(2,1)} custom-call(bf16[32,2,4,16,128]{4,3,2,1,0:T(8,128)(2,1)} %copy-done), custom_call_target="tpu_custom_call" | custom-call | tf_op jit(solution)/shard_map/triangle_product/pallas_call | solution.py:154
  117.6 5.7 %all-to-all-start.1 = ((bf16[32,4,16,128]{3,2,1,0:T(8,128)(2,1)}), bf16[32,4,16,128]{3,2,1,0:T(8,128)(2,1)S(1)}, u32[]{:S(2)}, u32[]{:S(2)}) async-start(bf16[32,4,16,128]{3,2,1,0:T(8,128)(2,1)} %triangle_product.1), calls=%async_computation.1 | async-start | bytes 1048576 | tf_op jit(solution)/shard_map/all_to_all | solution.py:471
  123.5 2.7 %reshape.82 = f32[8,16,64,32]{3,2,1,0:T(8,128)} reshape(f32[8,16,2048]{2,1,0:T(8,128)S(1)} %convert_add_fusion) | data formatting | bytes 2097152 | tf_op jit(solution)/shard_map/reshape | solution.py:462
  126.2 2.9 %copy.50 = f32[8,16,64,32]{2,3,1,0:T(8,128)S(1)} copy(f32[8,16,64,32]{3,2,1,0:T(8,128)} %reshape.82) | data formatting | bytes 2097152 | tf_op jit(solution)/shard_map/reshape | solution.py:462
  129.1 2.0 %fusion.7 = bf16[64,16,64]{2,0,1:T(8,128)(2,1)S(1)} fusion(bf16[8,32,64,1]{2,1,3,0:T(8,128)(2,1)S(1)} %bitcast.70, f32[8,16,64,32]{2,3,1,0:T(8,128)S(1)} %copy.50, f32[8,16]{1,0:T(8,128)S(1)} %copy.51, bf16[64,8,32,1]{0,2,3,1:T(8,128)(2,1)S(1)} %bitcast.71, bf16[16,64,64]{2,1,0:T(8,128)(2,1)} %get-tuple-element.17, bf16[16,64,64]{2,1,0:T(8,128)(2,1)S(1)} %copy-done.4), kind=kOutput, calls=%fused_computation.11 | convolution fusion | flops 68878336 | bytes 1507840 | tf_op jit(solution)/shard_map/hisc,hcm->sim/dot_general | solution.py:464
  131.1 0.9 copy.53
  132.0 6.1 %all-to-all-done.1.product_ref = bf16[32,4,16,128]{3,2,1,0:T(8,128)(2,1)S(1)} async-done(((bf16[32,4,16,128]{3,2,1,0:T(8,128)(2,1)}), bf16[32,4,16,128]{3,2,1,0:T(8,128)(2,1)S(1)}, u32[]{:S(2)}, u32[]{:S(2)}) %all-to-all-start.1) | async-done | bytes 524320 | tf_op jit(solution)/shard_map/all_to_all | solution.py:471
  138.2 0.8 copy-done.1
  139.0 9.4 %tail_stage.1 = bf16[16,128,128]{2,1,0:T(8,128)(2,1)} custom-call(bf16[32,4,16,128]{3,2,1,0:T(8,128)(2,1)} %copy-done.1, bf16[16,128,128]{2,1,0:T(8,128)(2,1)} %get-tuple-element.15.one_ref, f32[16,128,128]{2,1,0:T(8,128)} %fusion.4.gate_ref, bf16[128,128]{1,0:T(8,128)(2,1)} %mix_ref.1, bf16[128,1024]{1,0:T(8,128)(2,1)} %up_ref.1, bf16[512,128]{1,0:T(8,128)(2,1)} %down_ref.1), custom_call_target="tpu_custom_call" | custom-call | tf_op jit(solution)/shard_map/tail_stage/pallas_call | solution.py:373
  (37 shorter events, 1.1 us)
Async XLA Ops:
  0.6 24.2 %slice-start = ((bf16[128,640]{1,0:T(8,128)(2,1)}), bf16[128,512]{1,0:T(8,128)(2,1)S(1)}, s32[]{:S(2)}) async-start(bf16[128,640]{1,0:T(8,128)(2,1)} %param.22), calls=%async_computation.2 | async-start | bytes 262144 | tf_op jit(solution)/shard_map/slice | solution.py:300
  0.6 24.3 %copy-start.10 = (s32[256]{0:T(256)S(1)}, s32[256]{0:T(256)}, u32[]{:S(2)}) copy-start(s32[256]{0:T(256)} %param.16) | copy-start | bytes 3076
  0.7 24.4 %copy-start.8 = (bf16[128,8]{0,1:T(8,128)(2,1)S(1)}, bf16[128,8]{0,1:T(8,128)(2,1)}, u32[]{:S(2)}) copy-start(bf16[128,8]{0,1:T(8,128)(2,1)} %param.19) | copy-start | bytes 6148
  24.9 23.9 %copy-start.4 = (bf16[16,64,64]{2,1,0:T(8,128)(2,1)S(1)}, bf16[16,64,64]{2,1,0:T(8,128)(2,1)}, u32[]{:S(2)}) copy-start(bf16[16,64,64]{2,1,0:T(8,128)(2,1)} %get-tuple-element.18) | copy-start | bytes 393220
  40.9 72.0 %all-to-all-start = ((bf16[32,2,4,16,128]{4,3,2,1,0:T(8,128)(2,1)}), bf16[32,2,4,16,128]{4,3,2,1,0:T(8,128)(2,1)S(1)}, u32[]{:S(2)}, u32[]{:S(2)}) async-start(bf16[32,2,4,16,128]{4,3,2,1,0:T(8,128)(2,1)} %get-tuple-element.14), calls=%async_computation | async-start | bytes 2097152 | tf_op jit(solution)/shard_map/all_to_all | solution.py:433
  80.1 2.2 %copy-start.6 = (bf16[64,512]{1,0:T(8,128)(2,1)S(1)}, bf16[64,512]{1,0:T(8,128)(2,1)}, u32[]{:S(2)}) copy-start(bf16[64,512]{1,0:T(8,128)(2,1)} %param.20) | copy-start | bytes 196612
  83.7 0.9 copy-start.3
  84.6 15.5 %copy-start.2 = (bf16[128,640]{1,0:T(8,128)(2,1)S(1)}, bf16[128,640]{1,0:T(8,128)(2,1)}, u32[]{:S(2)}) copy-start(bf16[128,640]{1,0:T(8,128)(2,1)} %param.22) | copy-start | bytes 491524
  84.7 15.5 %copy-start.9 = (bf16[16,128,128]{2,1,0:T(8,128)(2,1)S(1)}, bf16[16,128,128]{2,1,0:T(8,128)(2,1)}, u32[]{:S(2)}) copy-start(bf16[16,128,128]{2,1,0:T(8,128)(2,1)} %get-tuple-element.16) | copy-start | bytes 1572868
  86.7 36.7 %collective-permute-start = (bf16[8,16,2048]{2,1,0:T(8,128)(2,1)}, bf16[8,16,2048]{2,1,0:T(8,128)(2,1)S(1)}, u32[]{:S(2)}, u32[]{:S(2)}) collective-permute-start(bf16[8,16,2048]{2,1,0:T(8,128)(2,1)} %get-tuple-element.32), channel_id=1, source_target_pairs={{0,1},{1,0},{2,3},{3,2},{4,5},{5,4},{6,7},{7,6},{8,9},{9,8},{10,11... | collective-permute-start | bytes 1572872 | tf_op jit(solution)/shard_map/ppermute | solution.py:130
  100.1 12.7 %collective-permute-start.1 = (f32[8,16]{0,1:T(8,128)S(1)}, f32[8,16]{0,1:T(8,128)S(1)}, u32[]{:S(2)}, u32[]{:S(2)}) collective-permute-start(f32[8,16]{0,1:T(8,128)S(1)} %bitcast_reduce_fusion), channel_id=1, source_target_pairs={{0,1},{1,0},{2,3},{3,2},{4,5},{5,4},{6,7},{7,6},{8,9},{9,8},{10,11... | collective-permute-start | bytes 1544 | tf_op jit(solution)/shard_map/ppermute | solution.py:130
  100.2 1.4 copy-start.7
  112.9 1.0 copy-start
  117.6 20.5 %all-to-all-start.1 = ((bf16[32,4,16,128]{3,2,1,0:T(8,128)(2,1)}), bf16[32,4,16,128]{3,2,1,0:T(8,128)(2,1)S(1)}, u32[]{:S(2)}, u32[]{:S(2)}) async-start(bf16[32,4,16,128]{3,2,1,0:T(8,128)(2,1)} %triangle_product.1), calls=%async_computation.1 | async-start | bytes 1048576 | tf_op jit(solution)/shard_map/all_to_all | solution.py:471
  126.2 2.9 %copy-start.5 = (bf16[64,256]{0,1:T(8,128)(2,1)S(1)}, bf16[64,256]{0,1:T(8,128)(2,1)}, u32[]{:S(2)}) copy-start(bf16[64,256]{0,1:T(8,128)(2,1)} %copy.62) | copy-start | bytes 98308
  138.1 0.8 copy-start.1

commit v3 on v2

--- a/solution.py
+++ b/solution.py
@@ -14,10 +14,12 @@
     values = values.astype(jnp.float32)
     centred = values - jnp.mean(values, axis=channel_dim, keepdims=True)
     spread = jnp.mean(centred * centred, axis=channel_dim, keepdims=True)
-    return centred / jnp.sqrt(spread + epsilon)
-
-
-def gather_kernel(n_row, n_col, block_ref, out_ref, own_sem, send_sems, far_sems, recv_sems):
+    return centred * lax.rsqrt(spread + epsilon)
+
+
+def gather_kernel(n_row, n_col, count, *refs):
+    blocks, outs = refs[:count], refs[count : 2 * count]
+    own_sem, send_sems, far_sems, recv_sems = refs[2 * count :]
     span = n_row // n_col
     row = lax.axis_index("row")
     col = lax.axis_index("col")
@@ -43,82 +45,92 @@
         pl.semaphore_signal(barrier, inc=1, device_id={"row": base + peer_place(k)})
     pl.semaphore_wait(barrier, n_col - 1 + half)
 
-    def push(source, slot, sem, recv, target):
+    def push(n, source, slot, sem, target):
         return pltpu.make_async_remote_copy(
             src_ref=source,
-            dst_ref=out_ref.at[slot],
+            dst_ref=outs[n].at[slot],
             send_sem=sem,
-            recv_sem=recv,
+            recv_sem=recv_sems.at[n, slot],
             device_id={"row": target},
         )
 
-    def far(k):
-        return push(block_ref, place, far_sems.at[k - 1], recv_sems.at[place], other_band(k))
+    def far(n, k):
+        return push(n, blocks[n], place, far_sems.at[n, k - 1], other_band(k))
+
+    def own_copy(n):
+        return pltpu.make_async_copy(blocks[n], outs[n].at[place], own_sem.at[n])
+
+    def arrival(n, slot):
+        return push(n, outs[n].at[place], slot, own_sem.at[n], base + twin_place)
 
     @pl.when(is_source)
     def _():
-        for k in range(1, n_col):
-            far(k).start()
-        own = pltpu.make_async_copy(block_ref, out_ref.at[place], own_sem)
-        own.start()
-        own.wait()
-
-    @pl.when(jnp.logical_not(is_source))
-    def _():
-        push(block_ref, place, own_sem, recv_sems.at[place], base + twin_place).wait_recv()
-
-    mine = out_ref.at[place]
-    near = [
-        push(mine, place, send_sems.at[k - 1], recv_sems.at[place], base + peer_place(k))
-        for k in range(1, half)
-    ]
-    near.append(push(mine, place, send_sems.at[half - 1], recv_sems.at[place], base + twin_place))
-    for copy in near:
-        copy.start()
-    for k in range(1, half):
-        came = lax.rem(place - 2 * k + span, span)
-        push(mine, came, own_sem, recv_sems.at[came], base + twin_place).wait_recv()
-        onward = push(
-            out_ref.at[came],
-            came,
-            send_sems.at[half - 1 + k],
-            recv_sems.at[came],
-            base + twin_place,
-        )
-        onward.start()
-        near.append(onward)
-    for k in range(half):
-        came = lax.rem(twin_place + 2 * k, span)
-        push(mine, came, own_sem, recv_sems.at[came], base + twin_place).wait_recv()
-    for copy in near:
+        for n in range(count):
+            for k in range(1, n_col):
+                far(n, k).start()
+            own_copy(n).start()
+        for n in range(count):
+            own_copy(n).wait()
+
+    sent = []
+    for n in range(count):
+
+        @pl.when(jnp.logical_not(is_source))
+        def _():
+            arrival(n, place).wait_recv()
+
+        mine = outs[n].at[place]
+        near = [
+            push(n, mine, place, send_sems.at[n, k - 1], base + peer_place(k))
+            for k in range(1, half)
+        ]
+        near.append(push(n, mine, place, send_sems.at[n, half - 1], base + twin_place))
+        for copy in near:
+            copy.start()
+        sent += near
+    for n in range(count):
+        for k in range(1, half):
+            came = lax.rem(place - 2 * k + span, span)
+            arrival(n, came).wait_recv()
+            onward = push(
+                n, outs[n].at[came], came, send_sems.at[n, half - 1 + k], base + twin_place
+            )
+            onward.start()
+            sent.append(onward)
+    for n in range(count):
+        for k in range(half):
+            arrival(n, lax.rem(twin_place + 2 * k, span)).wait_recv()
+    for copy in sent:
         copy.wait_send()
 
     @pl.when(is_source)
     def _():
-        for k in range(1, n_col):
-            far(k).wait_send()
-
-
-def gather_blocks(block, collective_id):
+        for n in range(count):
+            for k in range(1, n_col):
+                far(n, k).wait_send()
+
+
+def gather_blocks(*blocks):
     n_row = lax.axis_size("row")
     n_col = lax.axis_size("col")
     span = n_row // n_col
+    count = len(blocks)
     return pl.pallas_call(
-        functools.partial(gather_kernel, n_row, n_col),
-        out_shape=jax.ShapeDtypeStruct((span,) + block.shape, block.dtype),
-        in_specs=[pl.BlockSpec(memory_space=pltpu.VMEM)],
-        out_specs=pl.BlockSpec(memory_space=pltpu.VMEM),
+        functools.partial(gather_kernel, n_row, n_col, count),
+        out_shape=tuple(
+            jax.ShapeDtypeStruct((span,) + block.shape, block.dtype) for block in blocks
+        ),
+        in_specs=[pl.BlockSpec(memory_space=pltpu.VMEM)] * count,
+        out_specs=tuple(pl.BlockSpec(memory_space=pltpu.VMEM) for _ in blocks),
         scratch_shapes=[
-            pltpu.SemaphoreType.DMA,
-            pltpu.SemaphoreType.DMA((span,)),
-            pltpu.SemaphoreType.DMA((max(n_col - 1, 1),)),
-            pltpu.SemaphoreType.DMA((span,)),
+            pltpu.SemaphoreType.DMA((count,)),
+            pltpu.SemaphoreType.DMA((count, span)),
+            pltpu.SemaphoreType.DMA((count, max(n_col - 1, 1))),
+            pltpu.SemaphoreType.DMA((count, span)),
         ],
-        compiler_params=pltpu.CompilerParams(
-            collective_id=collective_id, has_side_effects=True
-        ),
-        name=f"gather_{collective_id}",
-    )(block)
+        compiler_params=pltpu.CompilerParams(collective_id=0, has_side_effects=True),
+        name="gather_blocks",
+    )(*blocks)
 
 
 def sum_columns(values, wire_dtype):
@@ -168,28 +180,30 @@
 
 
 def prep_kernel(
-    index_ref, pool_ref, row_weight_ref, column_weight_ref, align_ref, norm_ref, row_ref, column_ref, held_ref
+    index_ref, pool_ref, proj_ref, align_ref, norm_ref, row_ref, column_ref, held_ref
 ):
     tok_row, align_width, stored = pool_ref.shape
     samples = align_ref.shape[1]
-    outer_width = row_weight_ref.shape[1]
+    outer_width = proj_ref.shape[1] // 2
     half = outer_width // 2
-    slots = lax.broadcasted_iota(jnp.int32, (2 * samples, stored), 1)
-    picks = (slots == index_ref[...]).astype(jnp.bfloat16)
+    slots = lax.broadcasted_iota(jnp.int32, (stored, samples), 0)
+    picks = (slots == index_ref[...]).astype(jnp.float32).T.astype(jnp.bfloat16)
     lanes = lax.broadcasted_iota(jnp.int32, (half, 2 * samples), 1)
+    row_weight = proj_ref[:, :outer_width]
+    column_weight = proj_ref[...].astype(jnp.float32).T[outer_width:].astype(jnp.bfloat16)
     for t in range(tok_row):
-        twice = lax.dot_general(
+        chosen = lax.dot_general(
             picks, pool_ref[t], (((1,), (1,)), ((), ())), preferred_element_type=jnp.float32
         )
-        normed = normalize(twice, 1).astype(jnp.bfloat16)
-        align_ref[t] = twice[:samples].astype(jnp.bfloat16)
-        norm_ref[t] = normed[:samples]
+        normed = normalize(chosen, 1).astype(jnp.bfloat16)
+        align_ref[t] = chosen.astype(jnp.bfloat16)
+        norm_ref[t] = normed
         row_ref[t * samples : (t + 1) * samples, :] = jnp.dot(
-            normed[:samples], row_weight_ref[...], preferred_element_type=jnp.float32
+            normed, row_weight, preferred_element_type=jnp.float32
         ).astype(jnp.bfloat16)
         factor = lax.dot_general(
-            column_weight_ref[...],
-            normed,
+            column_weight,
+            jnp.concatenate([normed, normed], axis=0),
             (((1,), (1,)), ((), ())),
             preferred_element_type=jnp.float32,
         )
@@ -207,7 +221,6 @@
     samples = sample_index.shape[0]
     outer_width = outer_proj.shape[1] // 2
     half = outer_width // 2
-    spread = jnp.concatenate([sample_index, sample_index])[:, None]
     return pl.pallas_call(
         prep_kernel,
         out_shape=(
@@ -218,12 +231,7 @@
         ),
         scratch_shapes=[pltpu.VMEM((tok_row * half, 2 * samples), jnp.float32)],
         name="prepare",
-    )(
-        spread,
-        alignment_pool.transpose(1, 2, 0),
-        outer_proj[:, :outer_width],
-        outer_proj[:, outer_width:].T,
-    )
+    )(sample_index[None, :], alignment_pool.transpose(1, 2, 0), outer_proj)
 
 
 def pair_kernel(
@@ -235,13 +243,17 @@
     row_ref,
     mix_ref,
     grid_ref,
-    weight_ref,
+    proj_ref,
+    logit_ref,
     mask_ref,
     one_ref,
     norm_ref,
     score_ref,
     factor_ref,
     held_ref,
+    wide_ref,
+    mixed_ref,
+    weight_ref,
 ):
     step = pl.program_id(0)
     pair_width = grid_ref.shape[2]
@@ -249,15 +261,39 @@
     half = outer_width // 2
     tok_row = steps * step_rows
     order = [side * half + d for d in range(half) for side in range(2)]
-    spread = jnp.dot(row_ref[...], mix_ref[...], preferred_element_type=jnp.float32).astype(
+
+    @pl.when(step == 0)
+    def _():
+        wide_ref[...] = mix_ref[...].astype(jnp.float32)
+        for d in range(outer_width):
+            mixed_ref[:, d * pair_width : (d + 1) * pair_width] = wide_ref[
+                pl.ds(d, outer_width, stride=outer_width), :
+            ].astype(jnp.bfloat16)
+        for n in range(4):
+            part = proj_ref[:, n * pair_width : (n + 1) * pair_width].astype(jnp.float32)
+            weight_ref[n * pair_width : (n + 1) * pair_width, :] = part.T.astype(jnp.bfloat16)
+        weight_ref[4 * pair_width :, :] = logit_ref[...].astype(jnp.float32).T.astype(jnp.bfloat16)
+
+    spread = jnp.dot(row_ref[...], mixed_ref[...], preferred_element_type=jnp.float32).astype(
         jnp.bfloat16
     )
+    updates = []
+    for first in range(0, step_rows, 2):
+        both = []
+        for k in range(first, min(first + 2, step_rows)):
+            piece = spread[k * samples : (k + 1) * samples]
+            both.append(
+                jnp.concatenate(
+                    [piece[:, d * pair_width : (d + 1) * pair_width] for d in order], axis=0
+                )
+            )
+        update = jnp.dot(
+            column_ref[...], jnp.concatenate(both, axis=1), preferred_element_type=jnp.float32
+        )
+        for k in range(len(both)):
+            updates.append(update[:, k * pair_width : (k + 1) * pair_width])
     for k in range(step_rows):
-        piece = spread[k * samples : (k + 1) * samples]
-        stacked = jnp.concatenate(
-            [piece[:, d * pair_width : (d + 1) * pair_width] for d in order], axis=0
-        )
-        update = jnp.dot(column_ref[...], stacked, preferred_element_type=jnp.float32)
+        update = updates[k]
         pair_one = (grid_ref[k].astype(jnp.float32) + update * (1.0 / samples)).astype(jnp.bfloat16)
         one_ref[k] = pair_one
         pair_norm = normalize(pair_one, 1).astype(jnp.bfloat16)
@@ -293,11 +329,9 @@
     outer_width = rows.shape[1]
     samples = rows.shape[0] // tok_row
     head_count = pair_logit.shape[1]
-    step_rows = 2 if tok_row % 2 == 0 else 1
+    step_rows = 4 if tok_row % 4 == 0 else 1
     steps = tok_row // step_rows
     group = pair_width // devices
-    mix = outer_mix.reshape(outer_width, outer_width * pair_width)
-    weights = jnp.concatenate([triangle_proj[:, : 4 * pair_width], pair_logit], axis=1).T
     whole = lambda *shape: pl.BlockSpec(shape, lambda r: (0,) * len(shape))
     part = lambda *shape: pl.BlockSpec(shape, lambda r: (r,) + (0,) * (len(shape) - 1))
     return pl.pallas_call(
@@ -312,9 +346,10 @@
         in_specs=[
             whole(*columns.shape),
             part(step_rows * samples, outer_width),
-            whole(*mix.shape),
+            whole(*outer_mix.shape),
             part(step_rows, tok_col, pair_width),
-            whole(*weights.shape),
+            whole(*triangle_proj.shape),
+            whole(*pair_logit.shape),
             part(step_rows, 1, tok_col),
         ],
         out_specs=(
@@ -323,9 +358,14 @@
             part(step_rows, head_count, tok_col),
             whole(devices, 2, group, tok_row, tok_col),
         ),
-        scratch_shapes=[pltpu.VMEM((2, pair_width * tok_row, tok_col), jnp.float32)],
+        scratch_shapes=[
+            pltpu.VMEM((2, pair_width * tok_row, tok_col), jnp.float32),
+            pltpu.VMEM(outer_mix.shape, jnp.float32),
+            pltpu.VMEM((outer_width, outer_width * pair_width), jnp.bfloat16),
+            pltpu.VMEM((4 * pair_width + head_count, pair_width), jnp.bfloat16),
+        ],
         name="pair_stage",
-    )(columns, rows, mix, pair_grid, weights, pair_mask[:, None, :])
+    )(columns, rows, outer_mix, pair_grid, triangle_proj, pair_logit, pair_mask[:, None, :])
 
 
 def tail_kernel(
@@ -366,7 +406,7 @@
 
 def tail_stage(product, pair_one, gate_out, triangle_mix, transition_up, transition_down):
     tok_row, tok_col, pair_width = pair_one.shape
-    step_rows = 2 if tok_row % 2 == 0 else 1
+    step_rows = 4 if tok_row % 4 == 0 else 1
     whole = lambda *shape: pl.BlockSpec(shape, lambda r: (0,) * len(shape))
     part = lambda *shape: pl.BlockSpec(shape, lambda r: (r,) + (0,) * (len(shape) - 1))
     block = part(step_rows, tok_col, pair_width)
@@ -419,7 +459,9 @@
     column_mask = lax.dynamic_slice_in_dim(token_mask, column_start, tok_col, 0).astype(jnp.float32)
     pair_mask = row_mask[:, None] * column_mask[None, :]
     alignments, align_norm, rows, column_block = prepare(alignment_pool, sample_index, outer_proj)
-    columns = gather_blocks(column_block, 0).reshape(tok_col, column_block.shape[1])
+    align_rows = align_norm.transpose(1, 0, 2).reshape(samples, tok_row * align_width)
+    columns, gathered = gather_blocks(column_block, align_rows)
+    columns = columns.reshape(tok_col, column_block.shape[1])
     pair_one, pair_norm, weights, factors = pair_stage(
         columns,
         rows,
@@ -431,9 +473,6 @@
         n_row * n_col,
     )
     received = lax.all_to_all(factors, ("row", "col"), split_axis=0, concat_axis=0, tiled=True)
-    align_rows = align_norm.transpose(1, 0, 2).reshape(samples, tok_row * align_width)
-    align_rows, weights = lax.optimization_barrier((align_rows, weights))
-    gathered = gather_blocks(align_rows, 1)
     column_norm = (
         gathered.reshape(n_row // n_col, samples, tok_row, align_width)
         .transpose(1, 0, 2, 3)

time: 150 us -> 113 us (0.75)
  Pallas kernels: 72.4 us -> 45.6 us
  starting transfers between devices: 27 us -> 18.7 us
  local copies, waits for them, and re-layouts: 22.2 us -> 18.3 us
    pallas_call x2 -> x1, Pallas kernels: 38.2 us -> 19.1 us  [gather_blocks(): pl.pallas_call(functools.partial(gather_kernel, n_row, n_col, count), out...]
    ppermute x2, starting transfers between devices: 13.4 us -> 2.13 us  [sum_columns(): total = total + lax.ppermute(sent, 'col', pairs).astype(jnp.float32)]
    pallas_call x1, Pallas kernels: 14.5 us -> 9.32 us  [pair_stage(): pl.pallas_call(functools.partial(pair_kernel, steps, step_rows, samples,...]
    ppermute x2, waiting for transfers between devices: 10.4 us -> 13.5 us  [sum_columns(): total = total + lax.ppermute(sent, 'col', pairs).astype(jnp.float32)]
    pallas_call x1, Pallas kernels: 9.36 us -> 6.66 us  [tail_stage(): pl.pallas_call(functools.partial(tail_kernel, step_rows), grid=(tok_row /...]
    all_to_all x1, starting transfers between devices: 7.88 us -> 10.5 us  [on_device(): lax.all_to_all(factors, ('row', 'col'), split_axis=0, concat_axis=0, tile...]
    all_to_all x1, waiting for transfers between devices: 6.14 us -> 4.28 us  [on_device(): lax.all_to_all(flat_result, ('row', 'col'), split_axis=0, concat_axis=0,...]
    reshape x1 -> x0, local copies, waits for them, and re-layouts: 1.77 us -> none  [pair_stage(): mix = outer_mix.reshape(outer_width, outer_width * pair_width)]
  transfers between devices with their start and end apart: 4 -> 4, of which waited for: 2 -> 2; matrix products, arithmetic and copies ran while one was open for 15% -> 18% of each run, Pallas kernels for 20% -> 3%
where the time goes in v3:
time: 113 us; the launch traced here: 111 us
  Pallas kernels  45.6 us (40%)
  starting transfers between devices  18.7 us (17%)
  local copies, waits for them, and re-layouts  18.3 us (16%)
  waiting for transfers between devices  17.8 us (16%)
  matrix products  6.67 us (6%)
  other arithmetic  3.43 us (3%)
    pallas_call x1, Pallas kernels, gather_blocks(): pl.pallas_call(functools.partial(gather_kernel, n_row, n_col, count), out...  19.1 us
    ppermute x2, waiting for transfers between devices, sum_columns(): total = total + lax.ppermute(sent, 'col', pairs).astype(jnp.float32)  13.5 us
    all_to_all x1, starting transfers between devices, on_device(): lax.all_to_all(factors, ('row', 'col'), split_axis=0, concat_axis=0, tile...  10.5 us
    pallas_call x1, Pallas kernels, pair_stage(): pl.pallas_call(functools.partial(pair_kernel, steps, step_rows, samples,...  9.32 us
    pallas_call x1, Pallas kernels, prepare(): pl.pallas_call(prep_kernel, out_shape=(jax.ShapeDtypeStruct((tok_row, sam...  6.73 us
    pallas_call x1, Pallas kernels, tail_stage(): pl.pallas_call(functools.partial(tail_kernel, step_rows), grid=(tok_row /...  6.66 us
    all_to_all x1, starting transfers between devices, on_device(): lax.all_to_all(flat_result, ('row', 'col'), split_axis=0, concat_axis=0,...  6.1 us
    reshape x2, local copies, waits for them, and re-layouts, on_device(): weighted = weighted.reshape(head_count, tok_row, samples, head_dim)  5.6 us
  transfers between devices with their start and end apart: 4, of which 2 were waited for; matrix products, arithmetic and copies ran while one was open for 18% of the time, Pallas kernels for 3%

profile of v3, /device:TPU:0, one launch (start us, length us, event | category | flops | bytes accessed | tf_op | source)
XLA Modules:
  0.0 111.3 jit_solution(16394117256085701311)
XLA Ops:
  0.6 6.7 %prepare.1 = (bf16[16,64,64]{2,1,0:T(8,128)(2,1)}, bf16[16,64,64]{2,1,0:T(8,128)(2,1)}, bf16[1024,32]{1,0:T(8,128)(2,1)}, bf16[16,2048]{1,0:T(8,128)(2,1)}) custom-call(s32[1,64]{1,0:T(1,128)} %bitcast.68, bf16[16,64,256]{2,1,0:T(8,128)(2,1)} %bitcast.63, bf16[64,64]{1,0:T(8,128)(2,1)} %proj_ref.2), custom_call_target="tpu_custom_call" | custom-call | tf_op jit(solution)/shard_map/prepare/pallas_call | solution.py:224
  7.4 1.1 %copy.35 = bf16[64,16,64]{2,1,0:T(8,128)(2,1)S(1)} copy(bf16[64,16,64]{2,0,1:T(8,128)(2,1)} %bitcast.65) | data formatting | bytes 262144 | tf_op jit(solution)/shard_map/transpose | solution.py:462
  8.5 0.9 reshape.71.refs_1_
  9.4 1.4 %copy.36.logit_ref = bf16[128,8]{1,0:T(8,128)(2,1)} copy(bf16[128,8]{0,1:T(8,128)(2,1)} %param.19) | data formatting | bytes 4096 | tf_op args[6]
  10.7 0.8 dynamic-slice_convert_fusion
  11.5 0.8 dynamic-slice_convert_fusion.1
  12.2 19.1 %gather_blocks.1 = (bf16[8,16,2048]{2,1,0:T(8,128)(2,1)}, bf16[8,64,1024]{2,1,0:T(8,128)(2,1)}) custom-call(bf16[16,2048]{1,0:T(8,128)(2,1)} %get-tuple-element.12.refs_0_, bf16[64,1024]{1,0:T(8,128)(2,1)} %reshape.71.refs_1_), custom_call_target="tpu_custom_call" | custom-call | tf_op jit(solution)/shard_map/gather_blocks/pallas_call | solution.py:118
  31.4 0.7 broadcast_multiply_fusion.mask_ref
  32.1 9.3 %pair_stage.1 = (bf16[16,128,128]{2,1,0:T(8,128)(2,1)}, bf16[16,128,128]{2,1,0:T(8,128)(2,1)}, f32[16,8,128]{2,1,0:T(8,128)}, bf16[32,2,4,16,128]{4,3,2,1,0:T(8,128)(2,1)}) custom-call(bf16[128,2048]{1,0:T(8,128)(2,1)} %bitcast.62, bf16[1024,32]{1,0:T(8,128)(2,1)} %get-tuple-element.15.row_ref, bf16[1024,128]{1,0:T(8,128)(2,1)} %mix_ref.2, ...), custom_call_target="tpu_custom_call" | custom-call | tf_op jit(solution)/shard_map/pair_stage/pallas_call | solution.py:337
  41.4 10.5 %all-to-all-start = ((bf16[32,2,4,16,128]{4,3,2,1,0:T(8,128)(2,1)}), bf16[32,2,4,16,128]{4,3,2,1,0:T(8,128)(2,1)S(1)}, u32[]{:S(2)}, u32[]{:S(2)}) async-start(bf16[32,2,4,16,128]{4,3,2,1,0:T(8,128)(2,1)} %get-tuple-element.16), calls=%async_computation | async-start | bytes 2097152 | tf_op jit(solution)/shard_map/all_to_all | solution.py:475
  51.9 2.3 %reshape.74 = bf16[8,64,16,64]{3,2,1,0:T(8,128)(2,1)} reshape(bf16[8,64,1024]{2,1,0:T(8,128)(2,1)S(1)} %copy-done.2) | data formatting | bytes 2097152 | tf_op jit(solution)/shard_map/reshape | solution.py:477
  54.2 2.2 %copy.38 = bf16[8,64,16,64]{3,2,0,1:T(8,128)(2,1)S(1)} copy(bf16[8,64,16,64]{3,2,1,0:T(8,128)(2,1)} %reshape.74) | data formatting | bytes 2097152 | tf_op jit(solution)/shard_map/reshape | solution.py:477
  56.6 1.3 %convert_bitcast_fusion = bf16[8,128,64,32]{1,3,0,2:T(8,128)(2,1)S(1)} fusion(bf16[64,128,64,1]{2,1,3,0:T(8,128)(2,1)S(1)} %bitcast.61, bf16[64,8,32,1]{0,2,1,3:T(8,128)(2,1)S(1)} %bitcast.64), kind=kOutput, calls=%fused_computation | convolution fusion | flops 270532608 | bytes 5275648 | tf_op jit(solution)/shard_map/sjm,mhc->hjsc/dot_general | solution.py:487
  57.9 0.9 copy.41
  58.8 1.2 %fusion.19 = (bf16[8,16,2048]{2,1,0:T(8,128)(2,1)S(1)}, f32[8,16,2048]{2,1,0:T(8,128)S(1)}) fusion(bf16[8,128,2048]{1,2,0:T(8,128)(2,1)S(1)} %bitcast.60, bf16[8,16,128]{2,0,1:T(8,128)(2,1)S(1)} %bitcast_convert_fusion), kind=kOutput, calls=%fused_computation.26 | convolution fusion | flops 67371008 | bytes 5799936 | tf_op jit(solution)/shard_map/hij,hjk->hik/dot_general | solution.py:493
  60.0 1.8 %collective-permute-start = (bf16[8,16,2048]{2,1,0:T(8,128)(2,1)S(1)}, bf16[8,16,2048]{2,1,0:T(8,128)(2,1)S(1)}, u32[]{:S(2)}, u32[]{:S(2)}) collective-permute-start(bf16[8,16,2048]{2,1,0:T(8,128)(2,1)S(1)} %get-tuple-element.30), channel_id=1, source_target_pairs={{0,1},{1,0},{2,3},{3,2},{4,5},{5,4},{6,7},{7,6},{8,9},{9,8},{10,11... | collective-permute-start | bytes 1572872 | tf_op jit(solution)/shard_map/ppermute | solution.py:142
  61.9 0.3 collective-permute-start.1
  62.2 2.2 %fusion.4.gate_ref = f32[16,128,128]{2,1,0:T(8,128)} fusion(bf16[16,128,128]{2,1,0:T(8,128)(2,1)S(1)} %copy-done.8, bf16[128,640]{1,0:T(8,128)(2,1)} %proj_ref.3), kind=kOutput, calls=%fused_computation.7 | convolution fusion | flops 67895296 | bytes 1605632 | tf_op jit(solution)/shard_map/dot_general | solution.py:512
  64.5 0.1 copy.54
  64.6 13.5 %collective-permute-done.1 = f32[8,16]{0,1:T(8,128)S(1)} collective-permute-done((f32[8,16]{0,1:T(8,128)S(1)}, f32[8,16]{0,1:T(8,128)S(1)}, u32[]{:S(2)}, u32[]{:S(2)}) %collective-permute-start.1) | collective-permute-done | bytes 544 | tf_op jit(solution)/shard_map/ppermute | solution.py:142
  78.2 1.0 copy-done
  79.2 3.7 %triangle_product.1 = bf16[32,4,16,128]{3,2,1,0:T(8,128)(2,1)} custom-call(bf16[32,2,4,16,128]{4,3,2,1,0:T(8,128)(2,1)} %copy-done), custom_call_target="tpu_custom_call" | custom-call | tf_op jit(solution)/shard_map/triangle_product/pallas_call | solution.py:166
  82.9 6.1 %all-to-all-start.1 = ((bf16[32,4,16,128]{3,2,1,0:T(8,128)(2,1)}), bf16[32,4,16,128]{3,2,1,0:T(8,128)(2,1)S(1)}, u32[]{:S(2)}, u32[]{:S(2)}) async-start(bf16[32,4,16,128]{3,2,1,0:T(8,128)(2,1)} %triangle_product.1), calls=%async_computation.1 | async-start | bytes 1048576 | tf_op jit(solution)/shard_map/all_to_all | solution.py:510
  89.0 0.8 copy-done.3
  89.8 1.1 %convert_add_fusion = f32[8,16,2048]{2,1,0:T(8,128)S(1)} fusion(f32[8,16,2048]{2,1,0:T(8,128)S(1)} %get-tuple-element.31, bf16[8,16,2048]{2,1,0:T(8,128)(2,1)} %copy-done.3), kind=kLoop, calls=%fused_computation.12 | loop fusion | flops 524288 | bytes 2621440 | tf_op jit(solution)/shard_map/add | solution.py:142
  91.0 2.7 %reshape.78 = f32[8,16,64,32]{3,2,1,0:T(8,128)} reshape(f32[8,16,2048]{2,1,0:T(8,128)S(1)} %convert_add_fusion) | data formatting | bytes 2097152 | tf_op jit(solution)/shard_map/reshape | solution.py:501
  93.7 2.9 %copy.44 = f32[8,16,64,32]{2,3,1,0:T(8,128)S(1)} copy(f32[8,16,64,32]{3,2,1,0:T(8,128)} %reshape.78) | data formatting | bytes 2097152 | tf_op jit(solution)/shard_map/reshape | solution.py:501
  96.6 2.0 %fusion.7 = bf16[64,16,64]{2,0,1:T(8,128)(2,1)S(1)} fusion(bf16[8,32,64,1]{2,1,3,0:T(8,128)(2,1)S(1)} %bitcast.66, f32[8,16,64,32]{2,3,1,0:T(8,128)S(1)} %copy.44, f32[8,16]{1,0:T(8,128)S(1)} %copy.45, bf16[64,8,32,1]{0,2,3,1:T(8,128)(2,1)S(1)} %bitcast.67, bf16[16,64,64]{2,1,0:T(8,128)(2,1)} %get-tuple-element.19, bf16[16,64,64]{2,1,0:T(8,128)(2,1)S(1)} %copy-done.5), kind=kOutput, calls=%fused_computation.11 | convolution fusion | flops 68878336 | bytes 1507840 | tf_op jit(solution)/shard_map/hisc,hcm->sim/dot_general | solution.py:503
  98.6 0.9 copy.47
  99.5 4.3 %all-to-all-done.1.product_ref = bf16[32,4,16,128]{3,2,1,0:T(8,128)(2,1)S(1)} async-done(((bf16[32,4,16,128]{3,2,1,0:T(8,128)(2,1)}), bf16[32,4,16,128]{3,2,1,0:T(8,128)(2,1)S(1)}, u32[]{:S(2)}, u32[]{:S(2)}) %all-to-all-start.1) | async-done | bytes 524320 | tf_op jit(solution)/shard_map/all_to_all | solution.py:510
  103.8 0.8 copy-done.1
  104.6 6.7 %tail_stage.1 = bf16[16,128,128]{2,1,0:T(8,128)(2,1)} custom-call(bf16[32,4,16,128]{3,2,1,0:T(8,128)(2,1)} %copy-done.1, bf16[16,128,128]{2,1,0:T(8,128)(2,1)} %get-tuple-element.17.one_ref, f32[16,128,128]{2,1,0:T(8,128)} %fusion.4.gate_ref, bf16[128,128]{1,0:T(8,128)(2,1)} %mix_ref.3, bf16[128,1024]{1,0:T(8,128)(2,1)} %up_ref.1, bf16[512,128]{1,0:T(8,128)(2,1)} %down_ref.1), custom_call_target="tpu_custom_call" | custom-call | tf_op jit(solution)/shard_map/tail_stage/pallas_call | solution.py:413
  (24 shorter events, 0.4 us)
Async XLA Ops:
  31.4 20.5 %copy-start.2 = (bf16[8,64,1024]{2,1,0:T(8,128)(2,1)S(1)}, bf16[8,64,1024]{2,1,0:T(8,128)(2,1)}, u32[]{:S(2)}) copy-start(bf16[8,64,1024]{2,1,0:T(8,128)(2,1)} %get-tuple-element.21) | copy-start | bytes 3145732
  41.4 36.8 %all-to-all-start = ((bf16[32,2,4,16,128]{4,3,2,1,0:T(8,128)(2,1)}), bf16[32,2,4,16,128]{4,3,2,1,0:T(8,128)(2,1)S(1)}, u32[]{:S(2)}, u32[]{:S(2)}) async-start(bf16[32,2,4,16,128]{4,3,2,1,0:T(8,128)(2,1)} %get-tuple-element.16), calls=%async_computation | async-start | bytes 2097152 | tf_op jit(solution)/shard_map/all_to_all | solution.py:475
  54.2 2.2 %copy-start.6 = (bf16[64,512]{1,0:T(8,128)(2,1)S(1)}, bf16[64,512]{1,0:T(8,128)(2,1)}, u32[]{:S(2)}) copy-start(bf16[64,512]{1,0:T(8,128)(2,1)} %param.20) | copy-start | bytes 196612
  57.9 0.9 copy-start.4
  58.8 3.4 %copy-start.8 = (bf16[16,128,128]{2,1,0:T(8,128)(2,1)S(1)}, bf16[16,128,128]{2,1,0:T(8,128)(2,1)}, u32[]{:S(2)}) copy-start(bf16[16,128,128]{2,1,0:T(8,128)(2,1)} %get-tuple-element.18) | copy-start | bytes 1572868
  60.0 29.0 %collective-permute-start = (bf16[8,16,2048]{2,1,0:T(8,128)(2,1)S(1)}, bf16[8,16,2048]{2,1,0:T(8,128)(2,1)S(1)}, u32[]{:S(2)}, u32[]{:S(2)}) collective-permute-start(bf16[8,16,2048]{2,1,0:T(8,128)(2,1)S(1)} %get-tuple-element.30), channel_id=1, source_target_pairs={{0,1},{1,0},{2,3},{3,2},{4,5},{5,4},{6,7},{7,6},{8,9},{9,8},{10,11... | collective-permute-start | bytes 1572872 | tf_op jit(solution)/shard_map/ppermute | solution.py:142
  61.9 16.2 %collective-permute-start.1 = (f32[8,16]{0,1:T(8,128)S(1)}, f32[8,16]{0,1:T(8,128)S(1)}, u32[]{:S(2)}, u32[]{:S(2)}) collective-permute-start(f32[8,16]{0,1:T(8,128)S(1)} %bitcast_reduce_fusion), channel_id=1, source_target_pairs={{0,1},{1,0},{2,3},{3,2},{4,5},{5,4},{6,7},{7,6},{8,9},{9,8},{10,11... | collective-permute-start | bytes 1544 | tf_op jit(solution)/shard_map/ppermute | solution.py:142
  62.2 2.2 %copy-start.7 = (bf16[256,64]{0,1:T(8,128)(2,1)S(1)}, bf16[256,64]{0,1:T(8,128)(2,1)}, u32[]{:S(2)}) copy-start(bf16[256,64]{0,1:T(8,128)(2,1)} %param.21) | copy-start | bytes 98308
  78.2 1.0 copy-start
  82.9 20.9 %all-to-all-start.1 = ((bf16[32,4,16,128]{3,2,1,0:T(8,128)(2,1)}), bf16[32,4,16,128]{3,2,1,0:T(8,128)(2,1)S(1)}, u32[]{:S(2)}, u32[]{:S(2)}) async-start(bf16[32,4,16,128]{3,2,1,0:T(8,128)(2,1)} %triangle_product.1), calls=%async_computation.1 | async-start | bytes 1048576 | tf_op jit(solution)/shard_map/all_to_all | solution.py:510
  89.0 0.8 copy-start.3
  93.7 2.9 %copy-start.5 = (bf16[16,64,64]{2,1,0:T(8,128)(2,1)S(1)}, bf16[16,64,64]{2,1,0:T(8,128)(2,1)}, u32[]{:S(2)}) copy-start(bf16[16,64,64]{2,1,0:T(8,128)(2,1)} %get-tuple-element.13) | copy-start | bytes 393220
  103.8 0.8 copy-start.1

commit v4 on v3

--- a/solution.py
+++ b/solution.py
@@ -143,40 +143,106 @@
     return total
 
 
-def product_kernel(n_row, n_col, tok_row, tok_col, received_ref, out_ref, left_ref, right_ref):
-    for r in range(n_row):
-        for u in range(n_col):
-            rows = slice(r * tok_row, (r + 1) * tok_row)
-            lanes = slice(u * tok_col, (u + 1) * tok_col)
-            left_ref[rows, lanes] = received_ref[r * n_col + u, 0, 0]
-            right_ref[rows, lanes] = received_ref[r * n_col + u, 1, 0]
-    result = lax.dot_general(
-        left_ref[...], right_ref[...], (((1,), (1,)), ((), ())), preferred_element_type=jnp.float32
-    ).astype(jnp.bfloat16)
-    for r in range(n_row):
-        for u in range(n_col):
-            rows = slice(r * tok_row, (r + 1) * tok_row)
-            lanes = slice(u * tok_col, (u + 1) * tok_col)
-            out_ref[r * n_col + u, 0] = result[rows, lanes]
-
-
-def triangle_product(received, n_row, n_col):
-    devices, _, items, tok_row, tok_col = received.shape
-    length = n_row * tok_row
+def exchange_kernel(
+    n_row,
+    n_col,
+    sent_ref,
+    out_ref,
+    received_ref,
+    left_ref,
+    right_ref,
+    own_sem,
+    send_sems,
+    recv_sems,
+):
+    devices = n_row * n_col
+    me = lax.axis_index("row") * n_col + lax.axis_index("col")
+    barrier = pltpu.get_barrier_semaphore()
+
+    def place(k):
+        target = lax.rem(me + k, devices)
+        return {"row": target // n_col, "col": lax.rem(target, n_col)}
+
+    def greet(k, carry):
+        pl.semaphore_signal(barrier, inc=1, device_id=place(k))
+        return carry
+
+    def outgoing(k):
+        return pltpu.make_async_remote_copy(
+            src_ref=sent_ref.at[lax.rem(me + k, devices)],
+            dst_ref=received_ref.at[me],
+            send_sem=send_sems.at[k],
+            recv_sem=recv_sems.at[k],
+            device_id=place(k),
+        )
+
+    def incoming(k):
+        return pltpu.make_async_remote_copy(
+            src_ref=sent_ref.at[me],
+            dst_ref=received_ref.at[lax.rem(me - k + devices, devices)],
+            send_sem=send_sems.at[k],
+            recv_sem=recv_sems.at[k],
+            device_id=place(k),
+        )
+
+    def start(k, carry):
+        outgoing(k).start()
+        return carry
+
+    def finish(k, carry):
+        outgoing(k).wait_send()
+        incoming(k).wait_recv()
+        return carry
+
+    own = pltpu.make_async_copy(sent_ref.at[me], received_ref.at[me], own_sem)
+    lax.fori_loop(1, devices, greet, 0)
+    own.start()
+    pl.semaphore_wait(barrier, devices - 1)
+    lax.fori_loop(1, devices, start, 0)
+    own.wait()
+    lax.fori_loop(1, devices, finish, 0)
+    _, _, items, tok_row, tok_col = received_ref.shape
+    for item in range(items):
+        for r in range(n_row):
+            for u in range(n_col):
+                rows = slice(r * tok_row, (r + 1) * tok_row)
+                lanes = slice(u * tok_col, (u + 1) * tok_col)
+                left_ref[rows, lanes] = received_ref[r * n_col + u, 0, item]
+                right_ref[rows, lanes] = received_ref[r * n_col + u, 1, item]
+        result = lax.dot_general(
+            left_ref[...],
+            right_ref[...],
+            (((1,), (1,)), ((), ())),
+            preferred_element_type=jnp.float32,
+        ).astype(jnp.bfloat16)
+        for r in range(n_row):
+            for u in range(n_col):
+                rows = slice(r * tok_row, (r + 1) * tok_row)
+                lanes = slice(u * tok_col, (u + 1) * tok_col)
+                out_ref[r * n_col + u, item] = result[rows, lanes]
+
+
+def exchange_product(factors):
+    n_row = lax.axis_size("row")
+    n_col = lax.axis_size("col")
+    devices, _, items, tok_row, tok_col = factors.shape
+    square = (n_row * tok_row, n_col * tok_col)
     return pl.pallas_call(
-        functools.partial(product_kernel, n_row, n_col, tok_row, tok_col),
-        grid=(items,),
+        functools.partial(exchange_kernel, n_row, n_col),
         out_shape=jax.ShapeDtypeStruct((devices, items, tok_row, tok_col), jnp.bfloat16),
-        in_specs=[
-            pl.BlockSpec((devices, 2, 1, tok_row, tok_col), lambda c: (0, 0, c, 0, 0))
+        in_specs=[pl.BlockSpec(memory_space=pltpu.VMEM)],
+        out_specs=pl.BlockSpec(memory_space=pltpu.VMEM),
+        scratch_shapes=[
+            pltpu.VMEM(factors.shape, jnp.bfloat16),
+            pltpu.VMEM(square, jnp.bfloat16),
+            pltpu.VMEM(square, jnp.bfloat16),
+            pltpu.SemaphoreType.DMA,
+            pltpu.SemaphoreType.DMA((devices,)),
+            pltpu.SemaphoreType.DMA((devices,)),
         ],
-        out_specs=pl.BlockSpec((devices, 1, tok_row, tok_col), lambda c: (0, c, 0, 0)),
-        scratch_shapes=[
-            pltpu.VMEM((length, length), jnp.bfloat16),
-            pltpu.VMEM((length, length), jnp.bfloat16),
-        ],
-        name="triangle_product",
-    )(received)
+        compiler_params=pltpu.CompilerParams(collective_id=1, has_side_effects=True),
+        name="exchange_product",
+    )(factors)
 
 
 def prep_kernel(
@@ -472,7 +538,8 @@
         pair_mask,
         n_row * n_col,
     )
-    received = lax.all_to_all(factors, ("row", "col"), split_axis=0, concat_axis=0, tiled=True)
+    flat_result = exchange_product(factors)
+    flat_result, weights, gathered = lax.optimization_barrier((flat_result, weights, gathered))
     column_norm = (
         gathered.reshape(n_row // n_col, samples, tok_row, align_width)
         .transpose(1, 0, 2, 3)
@@ -506,7 +573,6 @@
     alignment_next = (
         alignments.transpose(1, 0, 2).astype(jnp.float32) + align_update
     ).astype(jnp.bfloat16)
-    flat_result = triangle_product(received, n_row, n_col)
     product = lax.all_to_all(flat_result, ("row", "col"), split_axis=0, concat_axis=0, tiled=True)
     gate_out = jax.nn.sigmoid(
         jnp.dot(pair_norm, triangle_proj[:, 4 * pair_width :], preferred_element_type=jnp.float32)

time: 113 us -> 122 us (1.080)
  the two profiles are of different devices: /device:TPU:0 before, /device:TPU:14 now
where the time goes in v4:
time: 122 us
  Pallas kernels  77.8 us (64%)
  local copies, waits for them, and re-layouts  16.5 us (14%)
  waiting for transfers between devices  11.1 us (9%)
  matrix products  6.94 us (6%)
  starting transfers between devices  6.04 us (5%)
  other arithmetic  2.39 us (2%)
    pallas_call x1, Pallas kernels, exchange_product(): pl.pallas_call(functools.partial(exchange_kernel, n_row, n_col), out_shap...  30.8 us
    pallas_call x1, Pallas kernels, gather_blocks(): pl.pallas_call(functools.partial(gather_kernel, n_row, n_col, count), out...  24.3 us
    ppermute x2, waiting for transfers between devices, sum_columns(): total = total + lax.ppermute(sent, 'col', pairs).astype(jnp.float32)  11.1 us
    pallas_call x1, Pallas kernels, pair_stage(): pl.pallas_call(functools.partial(pair_kernel, steps, step_rows, samples,...  9.36 us
    pallas_call x1, Pallas kernels, prepare(): pl.pallas_call(prep_kernel, out_shape=(jax.ShapeDtypeStruct((tok_row, sam...  6.75 us
    pallas_call x1, Pallas kernels, tail_stage(): pl.pallas_call(functools.partial(tail_kernel, step_rows), grid=(tok_row /...  6.66 us
    reshape x2, local copies, waits for them, and re-layouts, on_device(): weighted = weighted.reshape(head_count, tok_row, samples, head_dim)  5.59 us
    all_to_all x1, starting transfers between devices, on_device(): lax.all_to_all(flat_result, ('row', 'col'), split_axis=0, concat_axis=0,...  5.37 us
  transfers between devices with their start and end apart: 3, of which 1 were waited for; matrix products, arithmetic and copies ran while one was open for 9% of the time, Pallas kernels for 0%

profile of v4, /device:TPU:14, one launch (start us, length us, event | category | flops | bytes accessed | tf_op | source)
XLA Modules:
  0.0 121.7 jit_solution(15790848807191628198)
XLA Ops:
  0.6 6.7 %prepare.1 = (bf16[16,64,64]{2,1,0:T(8,128)(2,1)}, bf16[16,64,64]{2,1,0:T(8,128)(2,1)}, bf16[1024,32]{1,0:T(8,128)(2,1)}, bf16[16,2048]{1,0:T(8,128)(2,1)}) custom-call(s32[1,64]{1,0:T(1,128)} %bitcast.68, bf16[16,64,256]{2,1,0:T(8,128)(2,1)} %bitcast.63, bf16[64,64]{1,0:T(8,128)(2,1)} %proj_ref.2), custom_call_target="tpu_custom_call" | custom-call | tf_op jit(solution)/shard_map/prepare/pallas_call | solution.py:290
  7.4 1.1 copy.35
  8.5 0.9 reshape.71.refs_1_
  9.4 1.4 %copy.36.logit_ref = bf16[128,8]{1,0:T(8,128)(2,1)} copy(bf16[128,8]{0,1:T(8,128)(2,1)} %param.19) | data formatting | bytes 4096 | tf_op args[6]
  10.8 0.8 dynamic-slice_convert_fusion
  11.5 0.8 dynamic-slice_convert_fusion.1
  12.3 24.3 %gather_blocks.1 = (bf16[8,16,2048]{2,1,0:T(8,128)(2,1)}, bf16[8,64,1024]{2,1,0:T(8,128)(2,1)}) custom-call(bf16[16,2048]{1,0:T(8,128)(2,1)} %get-tuple-element.15.refs_0_, bf16[64,1024]{1,0:T(8,128)(2,1)} %reshape.71.refs_1_), custom_call_target="tpu_custom_call" | custom-call | tf_op jit(solution)/shard_map/gather_blocks/pallas_call | solution.py:118
  36.6 0.7 broadcast_multiply_fusion.mask_ref
  37.2 9.4 %pair_stage.1 = (bf16[16,128,128]{2,1,0:T(8,128)(2,1)}, bf16[16,128,128]{2,1,0:T(8,128)(2,1)}, f32[16,8,128]{2,1,0:T(8,128)}, bf16[32,2,4,16,128]{4,3,2,1,0:T(8,128)(2,1)}) custom-call(bf16[128,2048]{1,0:T(8,128)(2,1)} %bitcast.62, bf16[1024,32]{1,0:T(8,128)(2,1)} %get-tuple-element.18.row_ref, bf16[1024,128]{1,0:T(8,128)(2,1)} %mix_ref.2, ...), custom_call_target="tpu_custom_call" | custom-call | tf_op jit(solution)/shard_map/pair_stage/pallas_call | solution.py:403
  46.6 30.8 %exchange_product.1 = bf16[32,4,16,128]{3,2,1,0:T(8,128)(2,1)} custom-call(bf16[32,2,4,16,128]{4,3,2,1,0:T(8,128)(2,1)} %get-tuple-element.19.sent_ref), custom_call_target="tpu_custom_call" | custom-call | tf_op jit(solution)/shard_map/exchange_product/pallas_call | solution.py:230
  77.4 2.3 %reshape.74 = bf16[8,64,16,64]{3,2,1,0:T(8,128)(2,1)} reshape(bf16[8,64,1024]{2,1,0:T(8,128)(2,1)S(1)} %copy-done.1) | data formatting | bytes 2097152 | tf_op jit(solution)/shard_map/reshape | solution.py:544
  79.7 2.2 %copy.38 = bf16[8,64,16,64]{3,2,0,1:T(8,128)(2,1)S(1)} copy(bf16[8,64,16,64]{3,2,1,0:T(8,128)(2,1)} %reshape.74) | data formatting | bytes 2097152 | tf_op jit(solution)/shard_map/reshape | solution.py:544
  82.0 0.1 copy.39
  82.1 1.3 %convert_bitcast_fusion = bf16[8,128,64,32]{1,3,0,2:T(8,128)(2,1)S(1)} fusion(bf16[64,128,64,1]{2,1,3,0:T(8,128)(2,1)S(1)} %bitcast.61, bf16[64,8,32,1]{0,2,1,3:T(8,128)(2,1)S(1)} %bitcast.64), kind=kOutput, calls=%fused_computation | convolution fusion | flops 270532608 | bytes 5275648 | tf_op jit(solution)/shard_map/sjm,mhc->hjsc/dot_general | solution.py:554
  83.4 0.9 copy.41
  84.3 1.2 fusion.19
  85.5 0.0 collective-permute-start
  85.5 5.4 %all-to-all-start = ((bf16[32,4,16,128]{3,2,1,0:T(8,128)(2,1)}), bf16[32,4,16,128]{3,2,1,0:T(8,128)(2,1)S(1)}, u32[]{:S(2)}, u32[]{:S(2)}) async-start(bf16[32,4,16,128]{3,2,1,0:T(8,128)(2,1)} %exchange_product.1), calls=%async_computation | async-start | bytes 1048576 | tf_op jit(solution)/shard_map/all_to_all | solution.py:576
  90.9 0.1 bitcast_reduce_fusion
  91.0 0.6 collective-permute-start.1
  91.7 2.4 %fusion.4.gate_ref = f32[16,128,128]{2,1,0:T(8,128)} fusion(bf16[16,128,128]{2,1,0:T(8,128)(2,1)} %get-tuple-element.24, bf16[128,640]{1,0:T(8,128)(2,1)} %proj_ref.3), kind=kOutput, calls=%fused_computation.7 | convolution fusion | flops 67895296 | bytes 1605632 | tf_op jit(solution)/shard_map/dot_general | solution.py:578
  94.1 0.1 copy.46
  94.2 0.1 copy.54
  94.3 11.1 %collective-permute-done.1 = f32[8,16]{0,1:T(8,128)S(1)} collective-permute-done((f32[8,16]{0,1:T(8,128)S(1)}, f32[8,16]{0,1:T(8,128)S(1)}, u32[]{:S(2)}, u32[]{:S(2)}) %collective-permute-start.1) | collective-permute-done | bytes 544 | tf_op jit(solution)/shard_map/ppermute | solution.py:142
  105.5 0.1 copy.45
  105.5 0.1 convert_add_fusion
  105.7 2.7 %reshape.78 = f32[8,16,64,32]{3,2,1,0:T(8,128)} reshape(f32[8,16,2048]{2,1,0:T(8,128)S(1)} %convert_add_fusion) | data formatting | bytes 2097152 | tf_op jit(solution)/shard_map/reshape | solution.py:568
  108.4 2.9 %copy.44 = f32[8,16,64,32]{2,3,1,0:T(8,128)S(1)} copy(f32[8,16,64,32]{3,2,1,0:T(8,128)} %reshape.78) | data formatting | bytes 2097152 | tf_op jit(solution)/shard_map/reshape | solution.py:568
  111.3 2.0 %fusion.7 = bf16[64,16,64]{2,0,1:T(8,128)(2,1)S(1)} fusion(bf16[8,32,64,1]{2,1,3,0:T(8,128)(2,1)S(1)} %bitcast.66, f32[8,16,64,32]{2,3,1,0:T(8,128)S(1)} %copy.44, f32[8,16]{1,0:T(8,128)S(1)} %copy.45, bf16[64,8,32,1]{0,2,3,1:T(8,128)(2,1)S(1)} %bitcast.67, bf16[16,64,64]{2,1,0:T(8,128)(2,1)} %get-tuple-element.25, bf16[16,64,64]{2,1,0:T(8,128)(2,1)S(1)} %copy-done.3), kind=kOutput, calls=%fused_computation.11 | convolution fusion | flops 68878336 | bytes 1507840 | tf_op jit(solution)/shard_map/hisc,hcm->sim/dot_general | solution.py:570
  113.3 0.9 copy.47
  114.2 0.8 copy-done
  115.0 6.7 %tail_stage.1 = bf16[16,128,128]{2,1,0:T(8,128)(2,1)} custom-call(bf16[32,4,16,128]{3,2,1,0:T(8,128)(2,1)} %copy-done, bf16[16,128,128]{2,1,0:T(8,128)(2,1)} %get-tuple-element.23.one_ref, f32[16,128,128]{2,1,0:T(8,128)} %fusion.4.gate_ref, bf16[128,128]{1,0:T(8,128)(2,1)} %mix_ref.3, bf16[128,1024]{1,0:T(8,128)(2,1)} %up_ref.1, bf16[512,128]{1,0:T(8,128)(2,1)} %down_ref.1), custom_call_target="tpu_custom_call" | custom-call | tf_op jit(solution)/shard_map/tail_stage/pallas_call | solution.py:479
  (16 shorter events, 0.0 us)
Async XLA Ops:
  36.6 40.8 %copy-start.1 = (bf16[8,64,1024]{2,1,0:T(8,128)(2,1)S(1)}, bf16[8,64,1024]{2,1,0:T(8,128)(2,1)}, u32[]{:S(2)}) copy-start(bf16[8,64,1024]{2,1,0:T(8,128)(2,1)} %get-tuple-element.27) | copy-start | bytes 3145732
  79.7 2.2 %copy-start.4 = (bf16[64,512]{1,0:T(8,128)(2,1)S(1)}, bf16[64,512]{1,0:T(8,128)(2,1)}, u32[]{:S(2)}) copy-start(bf16[64,512]{1,0:T(8,128)(2,1)} %param.20) | copy-start | bytes 196612
  83.4 0.9 copy-start.2
  85.5 20.0 %collective-permute-start = (bf16[8,16,2048]{2,1,0:T(8,128)(2,1)S(1)}, bf16[8,16,2048]{2,1,0:T(8,128)(2,1)S(1)}, u32[]{:S(2)}, u32[]{:S(2)}) collective-permute-start(bf16[8,16,2048]{2,1,0:T(8,128)(2,1)S(1)} %get-tuple-element.36), channel_id=1, source_target_pairs={{0,1},{1,0},{2,3},{3,2},{4,5},{5,4},{6,7},{7,6},{8,9},{9,8},{10,11... | collective-permute-start | bytes 1572872 | tf_op jit(solution)/shard_map/ppermute | solution.py:142
  85.5 28.6 %all-to-all-start = ((bf16[32,4,16,128]{3,2,1,0:T(8,128)(2,1)}), bf16[32,4,16,128]{3,2,1,0:T(8,128)(2,1)S(1)}, u32[]{:S(2)}, u32[]{:S(2)}) async-start(bf16[32,4,16,128]{3,2,1,0:T(8,128)(2,1)} %exchange_product.1), calls=%async_computation | async-start | bytes 1048576 | tf_op jit(solution)/shard_map/all_to_all | solution.py:576
  91.0 14.4 %collective-permute-start.1 = (f32[8,16]{0,1:T(8,128)S(1)}, f32[8,16]{0,1:T(8,128)S(1)}, u32[]{:S(2)}, u32[]{:S(2)}) collective-permute-start(f32[8,16]{0,1:T(8,128)S(1)} %bitcast_reduce_fusion), channel_id=1, source_target_pairs={{0,1},{1,0},{2,3},{3,2},{4,5},{5,4},{6,7},{7,6},{8,9},{9,8},{10,11... | collective-permute-start | bytes 1544 | tf_op jit(solution)/shard_map/ppermute | solution.py:142
  91.7 2.4 %copy-start.5 = (bf16[256,64]{0,1:T(8,128)(2,1)S(1)}, bf16[256,64]{0,1:T(8,128)(2,1)}, u32[]{:S(2)}) copy-start(bf16[256,64]{0,1:T(8,128)(2,1)} %param.21) | copy-start | bytes 98308
  108.4 2.9 %copy-start.3 = (bf16[16,64,64]{2,1,0:T(8,128)(2,1)S(1)}, bf16[16,64,64]{2,1,0:T(8,128)(2,1)}, u32[]{:S(2)}) copy-start(bf16[16,64,64]{2,1,0:T(8,128)(2,1)} %get-tuple-element.16) | copy-start | bytes 393220
  114.2 0.8 copy-start

commit v5 on v3

--- a/solution.py
+++ b/solution.py
@@ -180,7 +180,7 @@
 
 
 def prep_kernel(
-    index_ref, pool_ref, proj_ref, align_ref, norm_ref, row_ref, column_ref, held_ref
+    index_ref, pool_ref, proj_ref, align_ref, norm_ref, flat_ref, row_ref, column_ref, held_ref
 ):
     tok_row, align_width, stored = pool_ref.shape
     samples = align_ref.shape[1]
@@ -198,6 +198,7 @@
         normed = normalize(chosen, 1).astype(jnp.bfloat16)
         align_ref[t] = chosen.astype(jnp.bfloat16)
         norm_ref[t] = normed
+        flat_ref[:, t * align_width : (t + 1) * align_width] = normed
         row_ref[t * samples : (t + 1) * samples, :] = jnp.dot(
             normed, row_weight, preferred_element_type=jnp.float32
         ).astype(jnp.bfloat16)
@@ -226,6 +227,7 @@
         out_shape=(
             jax.ShapeDtypeStruct((tok_row, samples, align_width), jnp.bfloat16),
             jax.ShapeDtypeStruct((tok_row, samples, align_width), jnp.bfloat16),
+            jax.ShapeDtypeStruct((samples, tok_row * align_width), jnp.bfloat16),
             jax.ShapeDtypeStruct((tok_row * samples, outer_width), jnp.bfloat16),
             jax.ShapeDtypeStruct((tok_row, outer_width * samples), jnp.bfloat16),
         ),
@@ -245,6 +247,7 @@
     grid_ref,
     proj_ref,
     logit_ref,
+    mark_ref,
     mask_ref,
     one_ref,
     norm_ref,
@@ -272,8 +275,12 @@
         for n in range(4):
             part = proj_ref[:, n * pair_width : (n + 1) * pair_width].astype(jnp.float32)
             weight_ref[n * pair_width : (n + 1) * pair_width, :] = part.T.astype(jnp.bfloat16)
-        weight_ref[4 * pair_width :, :] = logit_ref[...].astype(jnp.float32).T.astype(jnp.bfloat16)
-
+        weight_ref[4 * pair_width :, :] = logit_ref[...]
+
+    tok_col = grid_ref.shape[1]
+    row_start = lax.axis_index("row") * tok_row
+    column_start = pl.multiple_of(lax.axis_index("col") * tok_col, tok_col)
+    column_mask = mask_ref[:, pl.ds(column_start, tok_col)].astype(jnp.float32)
     spread = jnp.dot(row_ref[...], mixed_ref[...], preferred_element_type=jnp.float32).astype(
         jnp.bfloat16
     )
@@ -304,8 +311,8 @@
             (((1,), (1,)), ((), ())),
             preferred_element_type=jnp.float32,
         )
-        mask = mask_ref[k]
         row = step * step_rows + k
+        mask = column_mask * mark_ref[row_start + row].astype(jnp.float32)
         for side in range(2):
             base = 2 * side * pair_width
             gate = projected[base : base + pair_width]
@@ -324,7 +331,7 @@
             )
 
 
-def pair_stage(columns, rows, outer_mix, pair_grid, triangle_proj, pair_logit, pair_mask, devices):
+def pair_stage(columns, rows, outer_mix, pair_grid, triangle_proj, pair_logit, token_mask, devices):
     tok_row, tok_col, pair_width = pair_grid.shape
     outer_width = rows.shape[1]
     samples = rows.shape[0] // tok_row
@@ -349,8 +356,9 @@
             whole(*outer_mix.shape),
             part(step_rows, tok_col, pair_width),
             whole(*triangle_proj.shape),
-            whole(*pair_logit.shape),
-            part(step_rows, 1, tok_col),
+            whole(*pair_logit.shape[::-1]),
+            pl.BlockSpec(memory_space=pltpu.SMEM),
+            whole(1, token_mask.shape[0]),
         ],
         out_specs=(
             part(step_rows, tok_col, pair_width),
@@ -365,7 +373,7 @@
             pltpu.VMEM((4 * pair_width + head_count, pair_width), jnp.bfloat16),
         ],
         name="pair_stage",
-    )(columns, rows, outer_mix, pair_grid, triangle_proj, pair_logit, pair_mask[:, None, :])
+    )(columns, rows, outer_mix, pair_grid, triangle_proj, pair_logit.T, token_mask, token_mask[None, :])
 
 
 def tail_kernel(
@@ -453,13 +461,9 @@
     head_count = pair_logit.shape[1]
     head_total = average_proj.shape[1] // 2
     head_dim = head_total // head_count
-    row_start = lax.axis_index("row") * tok_row
-    column_start = lax.axis_index("col") * tok_col
-    row_mask = lax.dynamic_slice_in_dim(token_mask, row_start, tok_row, 0).astype(jnp.float32)
-    column_mask = lax.dynamic_slice_in_dim(token_mask, column_start, tok_col, 0).astype(jnp.float32)
-    pair_mask = row_mask[:, None] * column_mask[None, :]
-    alignments, align_norm, rows, column_block = prepare(alignment_pool, sample_index, outer_proj)
-    align_rows = align_norm.transpose(1, 0, 2).reshape(samples, tok_row * align_width)
+    alignments, align_norm, align_rows, rows, column_block = prepare(
+        alignment_pool, sample_index, outer_proj
+    )
     columns, gathered = gather_blocks(column_block, align_rows)
     columns = columns.reshape(tok_col, column_block.shape[1])
     pair_one, pair_norm, weights, factors = pair_stage(
@@ -469,7 +473,7 @@
         pair_grid,
         triangle_proj,
         pair_logit,
-        pair_mask,
+        token_mask,
         n_row * n_col,
     )
     received = lax.all_to_all(factors, ("row", "col"), split_axis=0, concat_axis=0, tiled=True)
@@ -493,6 +497,10 @@
     partial_sum = jnp.einsum(
         "hij,hjk->hik", weights_low, column_values, preferred_element_type=jnp.float32
     )
+    partial_sum = partial_sum.astype(jnp.bfloat16)
+    received, partial_sum, partial_total = lax.optimization_barrier(
+        (received, partial_sum, partial_total)
+    )
     weighted = sum_columns(partial_sum, jnp.bfloat16)
     totals = sum_columns(partial_total, jnp.float32)
     gate_values = jax.nn.sigmoid(

time: 113 us -> 108 us (0.956)
  waiting for transfers between devices: 17.8 us -> 24 us
  local copies, waits for them, and re-layouts: 18.3 us -> 13.1 us
  other arithmetic: 3.43 us -> 0.22 us
  starting transfers between devices: 18.7 us -> 16.3 us
    all_to_all x1, waiting for transfers between devices: 0.01 us -> 18 us  [on_device(): lax.all_to_all(factors, ('row', 'col'), split_axis=0, concat_axis=0, tile...]
    ppermute x2, waiting for transfers between devices: 13.5 us -> 2.15 us  [sum_columns(): total = total + lax.ppermute(sent, 'col', pairs).astype(jnp.float32)]
    unnamed x22 -> x19, local copies, waits for them, and re-layouts: 5.07 us -> 1.92 us
    all_to_all x1, starting transfers between devices: 6.1 us -> 3.8 us  [on_device(): lax.all_to_all(flat_result, ('row', 'col'), split_axis=0, concat_axis=0,...]
    convert_element_type x2 -> x0, other arithmetic: 1.5 us -> none  [the longest x1 0.75 us: on_device(): lax.dynamic_slice_in_dim(token_mask, column_start, tok_col, 0)]
  transfers between devices with their start and end apart: 4 -> 4, of which waited for: 2 -> 3; matrix products, arithmetic and copies ran while one was open for 18% -> 18% of each run, Pallas kernels for 3% -> 3%
where the time goes in v5:
time: 108 us; the launch traced here: 107 us
  Pallas kernels  45.6 us (42%)
  waiting for transfers between devices  24 us (22%)
  starting transfers between devices  16.3 us (15%)
  local copies, waits for them, and re-layouts  13.1 us (12%)
  matrix products  6.64 us (6%)
    pallas_call x1, Pallas kernels, gather_blocks(): pl.pallas_call(functools.partial(gather_kernel, n_row, n_col, count), out...  19.1 us
    all_to_all x1, waiting for transfers between devices, on_device(): lax.all_to_all(factors, ('row', 'col'), split_axis=0, concat_axis=0, tile...  18 us
    all_to_all x1, starting transfers between devices, on_device(): lax.all_to_all(factors, ('row', 'col'), split_axis=0, concat_axis=0, tile...  10.4 us
    pallas_call x1, Pallas kernels, pair_stage(): pl.pallas_call(functools.partial(pair_kernel, steps, step_rows, samples,...  9.37 us
    pallas_call x1, Pallas kernels, prepare(): pl.pallas_call(prep_kernel, out_shape=(jax.ShapeDtypeStruct((tok_row, sam...  6.75 us
    pallas_call x1, Pallas kernels, tail_stage(): pl.pallas_call(functools.partial(tail_kernel, step_rows), grid=(tok_row /...  6.66 us
    reshape x2, local copies, waits for them, and re-layouts, on_device(): weighted = weighted.reshape(head_count, tok_row, samples, head_dim)  5.59 us
    reshape x2, local copies, waits for them, and re-layouts, on_device(): gathered.reshape(n_row // n_col, samples, tok_row, align_width)  4.56 us
  transfers between devices with their start and end apart: 4, of which 3 were waited for; matrix products, arithmetic and copies ran while one was open for 18% of the time, Pallas kernels for 3%

profile of v5, /device:TPU:0, one launch (start us, length us, event | category | flops | bytes accessed | tf_op | source)
XLA Modules:
  0.0 106.8 jit_solution(17162586941002265935)
XLA Ops:
  0.6 6.7 %prepare.1 = (bf16[16,64,64]{2,1,0:T(8,128)(2,1)}, bf16[16,64,64]{2,1,0:T(8,128)(2,1)}, bf16[64,1024]{1,0:T(8,128)(2,1)}, bf16[1024,32]{1,0:T(8,128)(2,1)}, bf16[16,2048]{1,0:T(8,128)(2,1)}) custom-call(s32[1,64]{1,0:T(1,128)} %bitcast.70, bf16[16,64,256]{2,1,0:T(8,128)(2,1)} %bitcast.63, bf16[64,64]{1,0:T(8,128)(2,1)} %proj_ref.2), custom_call_target="tpu_custom_call" | custom-call | tf_op jit(solution)/shard_map/prepare/pallas_call | solution.py:225
  7.4 19.1 %gather_blocks.1 = (bf16[8,16,2048]{2,1,0:T(8,128)(2,1)}, bf16[8,64,1024]{2,1,0:T(8,128)(2,1)}) custom-call(bf16[16,2048]{1,0:T(8,128)(2,1)} %get-tuple-element.16.refs_0_, bf16[64,1024]{1,0:T(8,128)(2,1)} %get-tuple-element.17.refs_1_), custom_call_target="tpu_custom_call" | custom-call | tf_op jit(solution)/shard_map/gather_blocks/pallas_call | solution.py:118
  26.5 9.4 %pair_stage.1 = (bf16[16,128,128]{2,1,0:T(8,128)(2,1)}, bf16[16,128,128]{2,1,0:T(8,128)(2,1)}, f32[16,8,128]{2,1,0:T(8,128)}, bf16[32,2,4,16,128]{4,3,2,1,0:T(8,128)(2,1)}) custom-call(bf16[128,2048]{1,0:T(8,128)(2,1)} %bitcast.64, bf16[1024,32]{1,0:T(8,128)(2,1)} %get-tuple-element.19.row_ref, bf16[1024,128]{1,0:T(8,128)(2,1)} %mix_ref.2, ...), custom_call_target="tpu_custom_call" | custom-call | tf_op jit(solution)/shard_map/pair_stage/pallas_call | solution.py:344
  35.9 10.4 %all-to-all-start = ((bf16[32,2,4,16,128]{4,3,2,1,0:T(8,128)(2,1)}), bf16[32,2,4,16,128]{4,3,2,1,0:T(8,128)(2,1)S(1)}, u32[]{:S(2)}, u32[]{:S(2)}) async-start(bf16[32,2,4,16,128]{4,3,2,1,0:T(8,128)(2,1)} %get-tuple-element.20), calls=%async_computation | async-start | bytes 2097152 | tf_op jit(solution)/shard_map/all_to_all | solution.py:479
  46.4 2.3 %reshape.30 = bf16[8,64,16,64]{3,2,1,0:T(8,128)(2,1)} reshape(bf16[8,64,1024]{2,1,0:T(8,128)(2,1)S(1)} %copy-done.2) | data formatting | bytes 2097152 | tf_op jit(solution)/shard_map/reshape | solution.py:481
  48.7 2.2 %copy.31 = bf16[8,64,16,64]{3,2,0,1:T(8,128)(2,1)S(1)} copy(bf16[8,64,16,64]{3,2,1,0:T(8,128)(2,1)} %reshape.30) | data formatting | bytes 2097152 | tf_op jit(solution)/shard_map/reshape | solution.py:481
  50.9 0.0 copy-done.4
  51.0 0.1 copy.32
  51.1 1.3 %convert_bitcast_fusion = bf16[8,128,64,32]{1,3,0,2:T(8,128)(2,1)S(1)} fusion(bf16[64,128,64,1]{2,1,3,0:T(8,128)(2,1)S(1)} %bitcast.62, bf16[64,8,32,1]{0,2,1,3:T(8,128)(2,1)S(1)} %bitcast.65), kind=kOutput, calls=%fused_computation | convolution fusion | flops 270532608 | bytes 5275648 | tf_op jit(solution)/shard_map/sjm,mhc->hjsc/dot_general | solution.py:491
  52.3 0.9 copy.34
  53.2 0.1 bitcast_reduce_fusion
  53.4 0.0 copy-start.6
  53.4 1.2 %convolution_convert_fusion = bf16[8,16,2048]{2,1,0:T(8,128)(2,1)S(1)} fusion(bf16[8,128,2048]{1,2,0:T(8,128)(2,1)S(1)} %bitcast.61, bf16[8,16,128]{2,0,1:T(8,128)(2,1)S(1)} %bitcast_convert_fusion), kind=kOutput, calls=%fused_computation.1 | convolution fusion | flops 67371008 | bytes 4751360 | tf_op jit(solution)/shard_map/hij,hjk->hik/dot_general | solution.py:497
  54.6 18.0 %all-to-all-done.received_ref = bf16[32,2,4,16,128]{4,3,2,1,0:T(8,128)(2,1)S(1)} async-done(((bf16[32,2,4,16,128]{4,3,2,1,0:T(8,128)(2,1)}), bf16[32,2,4,16,128]{4,3,2,1,0:T(8,128)(2,1)S(1)}, u32[]{:S(2)}, u32[]{:S(2)}) %all-to-all-start) | async-done | bytes 1048608 | tf_op jit(solution)/shard_map/all_to_all | solution.py:479
  72.6 1.5 %collective-permute-start = (bf16[8,16,2048]{2,1,0:T(8,128)(2,1)S(1)}, bf16[8,16,2048]{2,1,0:T(8,128)(2,1)S(1)}, u32[]{:S(2)}, u32[]{:S(2)}) collective-permute-start(bf16[8,16,2048]{2,1,0:T(8,128)(2,1)S(1)} %convolution_convert_fusion), channel_id=1, source_target_pairs={{0,1},{1,0},{2,3},{3,2},{4,5},{5,4},{6,7},{7,6},{8,9},{9,8},{10,11... | collective-permute-start | bytes 1572872 | tf_op jit(solution)/shard_map/ppermute | solution.py:142
  74.0 0.6 collective-permute-start.1
  74.6 2.2 %fusion.4.gate_ref = f32[16,128,128]{2,1,0:T(8,128)} fusion(bf16[16,128,128]{2,1,0:T(8,128)(2,1)S(1)} %copy-done.6, bf16[128,640]{1,0:T(8,128)(2,1)} %proj_ref.3), kind=kOutput, calls=%fused_computation.8 | convolution fusion | flops 67895296 | bytes 1605632 | tf_op jit(solution)/shard_map/dot_general | solution.py:520
  76.7 0.1 copy.40
  76.9 0.1 copy.48
  77.0 3.7 %triangle_product.1 = bf16[32,4,16,128]{3,2,1,0:T(8,128)(2,1)} custom-call(bf16[32,2,4,16,128]{4,3,2,1,0:T(8,128)(2,1)} %copy-done), custom_call_target="tpu_custom_call" | custom-call | tf_op jit(solution)/shard_map/triangle_product/pallas_call | solution.py:166
  80.7 3.8 %all-to-all-start.1 = ((bf16[32,4,16,128]{3,2,1,0:T(8,128)(2,1)}), bf16[32,4,16,128]{3,2,1,0:T(8,128)(2,1)S(1)}, u32[]{:S(2)}, u32[]{:S(2)}) async-start(bf16[32,4,16,128]{3,2,1,0:T(8,128)(2,1)} %triangle_product.1), calls=%async_computation.1 | async-start | bytes 1048576 | tf_op jit(solution)/shard_map/all_to_all | solution.py:518
  84.5 2.1 %collective-permute-done.1 = f32[8,16]{0,1:T(8,128)S(1)} collective-permute-done((f32[8,16]{0,1:T(8,128)S(1)}, f32[8,16]{0,1:T(8,128)S(1)}, u32[]{:S(2)}, u32[]{:S(2)}) %collective-permute-start.1) | collective-permute-done | bytes 544 | tf_op jit(solution)/shard_map/ppermute | solution.py:142
  86.7 0.1 copy.39
  86.8 0.0 collective-permute-done
  86.8 0.1 convert_add_fusion
  86.9 2.7 %reshape.35 = f32[8,16,64,32]{3,2,1,0:T(8,128)} reshape(f32[8,16,2048]{2,1,0:T(8,128)S(1)} %convert_add_fusion) | data formatting | bytes 2097152 | tf_op jit(solution)/shard_map/reshape | solution.py:509
  89.6 2.9 %copy.38 = f32[8,16,64,32]{2,3,1,0:T(8,128)S(1)} copy(f32[8,16,64,32]{3,2,1,0:T(8,128)} %reshape.35) | data formatting | bytes 2097152 | tf_op jit(solution)/shard_map/reshape | solution.py:509
  92.5 2.0 %fusion.7 = bf16[64,16,64]{2,0,1:T(8,128)(2,1)S(1)} fusion(bf16[8,32,64,1]{2,1,3,0:T(8,128)(2,1)S(1)} %bitcast.66, f32[8,16,64,32]{2,3,1,0:T(8,128)S(1)} %copy.38, f32[8,16]{1,0:T(8,128)S(1)} %copy.39, bf16[64,8,32,1]{0,2,3,1:T(8,128)(2,1)S(1)} %bitcast.67, bf16[16,64,64]{2,1,0:T(8,128)(2,1)S(1)} %copy-done.7, bf16[16,64,64]{2,1,0:T(8,128)(2,1)} %get-tuple-element.27), kind=kOutput, calls=%fused_computation.12 | convolution fusion | flops 68878336 | bytes 1507840 | tf_op jit(solution)/shard_map/hisc,hcm->sim/dot_general | solution.py:511
  94.5 0.9 copy.41
  95.4 3.9 %all-to-all-done.1.product_ref = bf16[32,4,16,128]{3,2,1,0:T(8,128)(2,1)S(1)} async-done(((bf16[32,4,16,128]{3,2,1,0:T(8,128)(2,1)}), bf16[32,4,16,128]{3,2,1,0:T(8,128)(2,1)S(1)}, u32[]{:S(2)}, u32[]{:S(2)}) %all-to-all-start.1) | async-done | bytes 524320 | tf_op jit(solution)/shard_map/all_to_all | solution.py:518
  99.3 0.8 copy-done.1
  100.1 6.7 %tail_stage.1 = bf16[16,128,128]{2,1,0:T(8,128)(2,1)} custom-call(bf16[32,4,16,128]{3,2,1,0:T(8,128)(2,1)} %copy-done.1, bf16[16,128,128]{2,1,0:T(8,128)(2,1)} %get-tuple-element.24.one_ref, f32[16,128,128]{2,1,0:T(8,128)} %fusion.4.gate_ref, bf16[128,128]{1,0:T(8,128)(2,1)} %mix_ref.3, bf16[128,1024]{1,0:T(8,128)(2,1)} %up_ref.1, bf16[512,128]{1,0:T(8,128)(2,1)} %down_ref.1), custom_call_target="tpu_custom_call" | custom-call | tf_op jit(solution)/shard_map/tail_stage/pallas_call | solution.py:421
  (16 shorter events, 0.0 us)
Async XLA Ops:
  26.5 19.8 %copy-start.2 = (bf16[8,64,1024]{2,1,0:T(8,128)(2,1)S(1)}, bf16[8,64,1024]{2,1,0:T(8,128)(2,1)}, u32[]{:S(2)}) copy-start(bf16[8,64,1024]{2,1,0:T(8,128)(2,1)} %get-tuple-element.22) | copy-start | bytes 3145732
  35.9 36.7 %all-to-all-start = ((bf16[32,2,4,16,128]{4,3,2,1,0:T(8,128)(2,1)}), bf16[32,2,4,16,128]{4,3,2,1,0:T(8,128)(2,1)S(1)}, u32[]{:S(2)}, u32[]{:S(2)}) async-start(bf16[32,2,4,16,128]{4,3,2,1,0:T(8,128)(2,1)} %get-tuple-element.20), calls=%async_computation | async-start | bytes 2097152 | tf_op jit(solution)/shard_map/all_to_all | solution.py:479
  48.7 2.2 %copy-start.4 = (bf16[64,512]{1,0:T(8,128)(2,1)S(1)}, bf16[64,512]{1,0:T(8,128)(2,1)}, u32[]{:S(2)}) copy-start(bf16[64,512]{1,0:T(8,128)(2,1)} %param.20) | copy-start | bytes 196612
  52.3 0.9 copy-start.3
  53.4 21.2 %copy-start.6 = (bf16[16,128,128]{2,1,0:T(8,128)(2,1)S(1)}, bf16[16,128,128]{2,1,0:T(8,128)(2,1)}, u32[]{:S(2)}) copy-start(bf16[16,128,128]{2,1,0:T(8,128)(2,1)} %get-tuple-element.25) | copy-start | bytes 1572868
  72.6 4.2 %copy-start = (bf16[32,2,4,16,128]{4,3,2,1,0:T(8,128)(2,1)}, bf16[32,2,4,16,128]{4,3,2,1,0:T(8,128)(2,1)S(1)}, u32[]{:S(2)}) copy-start(bf16[32,2,4,16,128]{4,3,2,1,0:T(8,128)(2,1)S(1)} %all-to-all-done.received_ref) | copy-start | bytes 3145732
  72.6 14.2 %collective-permute-start = (bf16[8,16,2048]{2,1,0:T(8,128)(2,1)S(1)}, bf16[8,16,2048]{2,1,0:T(8,128)(2,1)S(1)}, u32[]{:S(2)}, u32[]{:S(2)}) collective-permute-start(bf16[8,16,2048]{2,1,0:T(8,128)(2,1)S(1)} %convolution_convert_fusion), channel_id=1, source_target_pairs={{0,1},{1,0},{2,3},{3,2},{4,5},{5,4},{6,7},{7,6},{8,9},{9,8},{10,11... | collective-permute-start | bytes 1572872 | tf_op jit(solution)/shard_map/ppermute | solution.py:142
  74.0 12.7 %collective-permute-start.1 = (f32[8,16]{0,1:T(8,128)S(1)}, f32[8,16]{0,1:T(8,128)S(1)}, u32[]{:S(2)}, u32[]{:S(2)}) collective-permute-start(f32[8,16]{0,1:T(8,128)S(1)} %bitcast_reduce_fusion), channel_id=1, source_target_pairs={{0,1},{1,0},{2,3},{3,2},{4,5},{5,4},{6,7},{7,6},{8,9},{9,8},{10,11... | collective-permute-start | bytes 1544 | tf_op jit(solution)/shard_map/ppermute | solution.py:142
  74.6 2.2 %copy-start.5 = (bf16[256,64]{0,1:T(8,128)(2,1)S(1)}, bf16[256,64]{0,1:T(8,128)(2,1)}, u32[]{:S(2)}) copy-start(bf16[256,64]{0,1:T(8,128)(2,1)} %param.21) | copy-start | bytes 98308
  80.7 18.6 %all-to-all-start.1 = ((bf16[32,4,16,128]{3,2,1,0:T(8,128)(2,1)}), bf16[32,4,16,128]{3,2,1,0:T(8,128)(2,1)S(1)}, u32[]{:S(2)}, u32[]{:S(2)}) async-start(bf16[32,4,16,128]{3,2,1,0:T(8,128)(2,1)} %triangle_product.1), calls=%async_computation.1 | async-start | bytes 1048576 | tf_op jit(solution)/shard_map/all_to_all | solution.py:518
  89.6 2.9 %copy-start.7 = (bf16[16,64,64]{2,1,0:T(8,128)(2,1)S(1)}, bf16[16,64,64]{2,1,0:T(8,128)(2,1)}, u32[]{:S(2)}) copy-start(bf16[16,64,64]{2,1,0:T(8,128)(2,1)} %get-tuple-element.26) | copy-start | bytes 393220
  99.3 0.8 copy-start.1

commit v6 on v5

--- a/solution.py
+++ b/solution.py
@@ -515,9 +515,10 @@
         alignments.transpose(1, 0, 2).astype(jnp.float32) + align_update
     ).astype(jnp.bfloat16)
     flat_result = triangle_product(received, n_row, n_col)
+    flat_result, late_norm = lax.optimization_barrier((flat_result, pair_norm))
     product = lax.all_to_all(flat_result, ("row", "col"), split_axis=0, concat_axis=0, tiled=True)
     gate_out = jax.nn.sigmoid(
-        jnp.dot(pair_norm, triangle_proj[:, 4 * pair_width :], preferred_element_type=jnp.float32)
+        jnp.dot(late_norm, triangle_proj[:, 4 * pair_width :], preferred_element_type=jnp.float32)
     )
     pair_next = tail_stage(
         product, pair_one, gate_out, triangle_mix, transition_up, transition_down

time: 108 us -> 108 us (level)
    ppermute x2, waiting for transfers between devices: 2.15 us -> 6.25 us  [sum_columns(): total = total + lax.ppermute(sent, 'col', pairs).astype(jnp.float32)]
    all_to_all x1, waiting for transfers between devices: 3.9 us -> 0.01 us  [on_device(): lax.all_to_all(flat_result, ('row', 'col'), split_axis=0, concat_axis=0,...]
    ppermute x2, starting transfers between devices: 2.03 us -> 3.13 us  [sum_columns(): total = total + lax.ppermute(sent, 'col', pairs).astype(jnp.float32)]
  transfers between devices with their start and end apart: 4 -> 4, of which waited for: 3 -> 2; matrix products, arithmetic and copies ran while one was open for 18% -> 18% of each run, Pallas kernels for 3% -> 4%
where the time goes in v6:
time: 108 us; the launch traced here: 107 us
  Pallas kernels  45.7 us (42%)
  waiting for transfers between devices  24.2 us (22%)
  starting transfers between devices  16.6 us (15%)
  local copies, waits for them, and re-layouts  13.1 us (12%)
  matrix products  6.65 us (6%)
    pallas_call x1, Pallas kernels, gather_blocks(): pl.pallas_call(functools.partial(gather_kernel, n_row, n_col, count), out...  19.1 us
    all_to_all x1, waiting for transfers between devices, on_device(): lax.all_to_all(factors, ('row', 'col'), split_axis=0, concat_axis=0, tile...  18 us
    all_to_all x1, starting transfers between devices, on_device(): lax.all_to_all(factors, ('row', 'col'), split_axis=0, concat_axis=0, tile...  10.4 us
    pallas_call x1, Pallas kernels, pair_stage(): pl.pallas_call(functools.partial(pair_kernel, steps, step_rows, samples,...  9.37 us
    pallas_call x1, Pallas kernels, prepare(): pl.pallas_call(prep_kernel, out_shape=(jax.ShapeDtypeStruct((tok_row, sam...  6.75 us
    pallas_call x1, Pallas kernels, tail_stage(): pl.pallas_call(functools.partial(tail_kernel, step_rows), grid=(tok_row /...  6.66 us
    ppermute x2, waiting for transfers between devices, sum_columns(): total = total + lax.ppermute(sent, 'col', pairs).astype(jnp.float32)  6.25 us
    reshape x2, local copies, waits for them, and re-layouts, on_device(): weighted = weighted.reshape(head_count, tok_row, samples, head_dim)  5.59 us
  transfers between devices with their start and end apart: 4, of which 2 were waited for; matrix products, arithmetic and copies ran while one was open for 18% of the time, Pallas kernels for 4%

profile of v6, /device:TPU:0, one launch (start us, length us, event | category | flops | bytes accessed | tf_op | source)
XLA Modules:
  0.0 107.4 jit_solution(11932863456902540074)
XLA Ops:
  0.6 6.7 %prepare.1 = (bf16[16,64,64]{2,1,0:T(8,128)(2,1)}, bf16[16,64,64]{2,1,0:T(8,128)(2,1)}, bf16[64,1024]{1,0:T(8,128)(2,1)}, bf16[1024,32]{1,0:T(8,128)(2,1)}, bf16[16,2048]{1,0:T(8,128)(2,1)}) custom-call(s32[1,64]{1,0:T(1,128)} %bitcast.70, bf16[16,64,256]{2,1,0:T(8,128)(2,1)} %bitcast.63, bf16[64,64]{1,0:T(8,128)(2,1)} %proj_ref.2), custom_call_target="tpu_custom_call" | custom-call | tf_op jit(solution)/shard_map/prepare/pallas_call | solution.py:225
  7.4 19.1 %gather_blocks.1 = (bf16[8,16,2048]{2,1,0:T(8,128)(2,1)}, bf16[8,64,1024]{2,1,0:T(8,128)(2,1)}) custom-call(bf16[16,2048]{1,0:T(8,128)(2,1)} %get-tuple-element.18.refs_0_, bf16[64,1024]{1,0:T(8,128)(2,1)} %get-tuple-element.19.refs_1_), custom_call_target="tpu_custom_call" | custom-call | tf_op jit(solution)/shard_map/gather_blocks/pallas_call | solution.py:118
  26.5 9.4 %pair_stage.1 = (bf16[16,128,128]{2,1,0:T(8,128)(2,1)}, bf16[16,128,128]{2,1,0:T(8,128)(2,1)}, f32[16,8,128]{2,1,0:T(8,128)}, bf16[32,2,4,16,128]{4,3,2,1,0:T(8,128)(2,1)}) custom-call(bf16[128,2048]{1,0:T(8,128)(2,1)} %bitcast.64, bf16[1024,32]{1,0:T(8,128)(2,1)} %get-tuple-element.21.row_ref, bf16[1024,128]{1,0:T(8,128)(2,1)} %mix_ref.2, ...), custom_call_target="tpu_custom_call" | custom-call | tf_op jit(solution)/shard_map/pair_stage/pallas_call | solution.py:344
  35.9 10.4 %all-to-all-start = ((bf16[32,2,4,16,128]{4,3,2,1,0:T(8,128)(2,1)}), bf16[32,2,4,16,128]{4,3,2,1,0:T(8,128)(2,1)S(1)}, u32[]{:S(2)}, u32[]{:S(2)}) async-start(bf16[32,2,4,16,128]{4,3,2,1,0:T(8,128)(2,1)} %get-tuple-element.22), calls=%async_computation | async-start | bytes 2097152 | tf_op jit(solution)/shard_map/all_to_all | solution.py:479
  46.4 2.3 %reshape.30 = bf16[8,64,16,64]{3,2,1,0:T(8,128)(2,1)} reshape(bf16[8,64,1024]{2,1,0:T(8,128)(2,1)S(1)} %copy-done.2) | data formatting | bytes 2097152 | tf_op jit(solution)/shard_map/reshape | solution.py:481
  48.7 2.2 %copy.31 = bf16[8,64,16,64]{3,2,0,1:T(8,128)(2,1)S(1)} copy(bf16[8,64,16,64]{3,2,1,0:T(8,128)(2,1)} %reshape.30) | data formatting | bytes 2097152 | tf_op jit(solution)/shard_map/reshape | solution.py:481
  51.0 0.1 copy.32
  51.1 1.3 %convert_bitcast_fusion = bf16[8,128,64,32]{1,3,0,2:T(8,128)(2,1)S(1)} fusion(bf16[64,128,64,1]{2,1,3,0:T(8,128)(2,1)S(1)} %bitcast.62, bf16[64,8,32,1]{0,2,1,3:T(8,128)(2,1)S(1)} %bitcast.65), kind=kOutput, calls=%fused_computation | convolution fusion | flops 270532608 | bytes 5275648 | tf_op jit(solution)/shard_map/sjm,mhc->hjsc/dot_general | solution.py:491
  52.3 0.9 copy.34
  53.2 0.1 bitcast_reduce_fusion
  53.4 0.0 copy-start.5
  53.4 1.2 %convolution_convert_fusion = bf16[8,16,2048]{2,1,0:T(8,128)(2,1)S(1)} fusion(bf16[8,128,2048]{1,2,0:T(8,128)(2,1)S(1)} %bitcast.61, bf16[8,16,128]{2,0,1:T(8,128)(2,1)S(1)} %bitcast_convert_fusion), kind=kOutput, calls=%fused_computation.1 | convolution fusion | flops 67371008 | bytes 4751360 | tf_op jit(solution)/shard_map/hij,hjk->hik/dot_general | solution.py:497
  54.6 18.0 %all-to-all-done.received_ref = bf16[32,2,4,16,128]{4,3,2,1,0:T(8,128)(2,1)S(1)} async-done(((bf16[32,2,4,16,128]{4,3,2,1,0:T(8,128)(2,1)}), bf16[32,2,4,16,128]{4,3,2,1,0:T(8,128)(2,1)S(1)}, u32[]{:S(2)}, u32[]{:S(2)}) %all-to-all-start) | async-done | bytes 1048608 | tf_op jit(solution)/shard_map/all_to_all | solution.py:479
  72.6 1.5 %collective-permute-start = (bf16[8,16,2048]{2,1,0:T(8,128)(2,1)S(1)}, bf16[8,16,2048]{2,1,0:T(8,128)(2,1)S(1)}, u32[]{:S(2)}, u32[]{:S(2)}) collective-permute-start(bf16[8,16,2048]{2,1,0:T(8,128)(2,1)S(1)} %convolution_convert_fusion), channel_id=1, source_target_pairs={{0,1},{1,0},{2,3},{3,2},{4,5},{5,4},{6,7},{7,6},{8,9},{9,8},{10,11... | collective-permute-start | bytes 1572872 | tf_op jit(solution)/shard_map/ppermute | solution.py:142
  74.0 0.1 copy.40
  74.1 0.1 copy.48
  74.3 0.0 copy-done
  74.3 3.8 %triangle_product.1 = bf16[32,4,16,128]{3,2,1,0:T(8,128)(2,1)} custom-call(bf16[32,2,4,16,128]{4,3,2,1,0:T(8,128)(2,1)} %copy-done), custom_call_target="tpu_custom_call" | custom-call | tf_op jit(solution)/shard_map/triangle_product/pallas_call | solution.py:166
  78.1 3.0 %all-to-all-start.1 = ((bf16[32,4,16,128]{3,2,1,0:T(8,128)(2,1)}), bf16[32,4,16,128]{3,2,1,0:T(8,128)(2,1)S(1)}, u32[]{:S(2)}, u32[]{:S(2)}) async-start(bf16[32,4,16,128]{3,2,1,0:T(8,128)(2,1)} %triangle_product.1), calls=%async_computation.1 | async-start | bytes 1048576 | tf_op jit(solution)/shard_map/all_to_all | solution.py:519
  81.1 1.7 %collective-permute-start.1 = (f32[8,16]{0,1:T(8,128)S(1)}, f32[8,16]{0,1:T(8,128)S(1)}, u32[]{:S(2)}, u32[]{:S(2)}) collective-permute-start(f32[8,16]{0,1:T(8,128)S(1)} %bitcast_reduce_fusion), channel_id=1, source_target_pairs={{0,1},{1,0},{2,3},{3,2},{4,5},{5,4},{6,7},{7,6},{8,9},{9,8},{10,11... | collective-permute-start | bytes 1544 | tf_op jit(solution)/shard_map/ppermute | solution.py:142
  82.8 2.2 %fusion.4.gate_ref = f32[16,128,128]{2,1,0:T(8,128)} fusion(bf16[16,128,128]{2,1,0:T(8,128)(2,1)S(1)} %copy-done.6, bf16[128,640]{1,0:T(8,128)(2,1)} %proj_ref.3), kind=kOutput, calls=%fused_computation.8 | convolution fusion | flops 67895296 | bytes 1605632 | tf_op jit(solution)/shard_map/dot_general | solution.py:521
  85.0 6.2 %collective-permute-done.1 = f32[8,16]{0,1:T(8,128)S(1)} collective-permute-done((f32[8,16]{0,1:T(8,128)S(1)}, f32[8,16]{0,1:T(8,128)S(1)}, u32[]{:S(2)}, u32[]{:S(2)}) %collective-permute-start.1) | collective-permute-done | bytes 544 | tf_op jit(solution)/shard_map/ppermute | solution.py:142
  91.2 0.1 copy.39
  91.3 0.0 collective-permute-done
  91.3 0.1 convert_add_fusion
  91.4 2.7 %reshape.35 = f32[8,16,64,32]{3,2,1,0:T(8,128)} reshape(f32[8,16,2048]{2,1,0:T(8,128)S(1)} %convert_add_fusion) | data formatting | bytes 2097152 | tf_op jit(solution)/shard_map/reshape | solution.py:509
  94.2 2.9 %copy.38 = f32[8,16,64,32]{2,3,1,0:T(8,128)S(1)} copy(f32[8,16,64,32]{3,2,1,0:T(8,128)} %reshape.35) | data formatting | bytes 2097152 | tf_op jit(solution)/shard_map/reshape | solution.py:509
  97.0 2.0 %fusion.7 = bf16[64,16,64]{2,0,1:T(8,128)(2,1)S(1)} fusion(bf16[8,32,64,1]{2,1,3,0:T(8,128)(2,1)S(1)} %bitcast.66, f32[8,16,64,32]{2,3,1,0:T(8,128)S(1)} %copy.38, f32[8,16]{1,0:T(8,128)S(1)} %copy.39, bf16[64,8,32,1]{0,2,3,1:T(8,128)(2,1)S(1)} %bitcast.67, bf16[16,64,64]{2,1,0:T(8,128)(2,1)S(1)} %copy-done.7, bf16[16,64,64]{2,1,0:T(8,128)(2,1)} %get-tuple-element.31), kind=kOutput, calls=%fused_computation.12 | convolution fusion | flops 68878336 | bytes 1507840 | tf_op jit(solution)/shard_map/hisc,hcm->sim/dot_general | solution.py:511
  99.1 0.9 copy.41
  100.0 0.0 all-to-all-done.1.product_ref
  100.0 0.8 copy-done.1
  100.8 6.7 %tail_stage.1 = bf16[16,128,128]{2,1,0:T(8,128)(2,1)} custom-call(bf16[32,4,16,128]{3,2,1,0:T(8,128)(2,1)} %copy-done.1, bf16[16,128,128]{2,1,0:T(8,128)(2,1)} %get-tuple-element.28.one_ref, f32[16,128,128]{2,1,0:T(8,128)} %fusion.4.gate_ref, bf16[128,128]{1,0:T(8,128)(2,1)} %mix_ref.3, bf16[128,1024]{1,0:T(8,128)(2,1)} %up_ref.1, bf16[512,128]{1,0:T(8,128)(2,1)} %down_ref.1), custom_call_target="tpu_custom_call" | custom-call | tf_op jit(solution)/shard_map/tail_stage/pallas_call | solution.py:421
  (16 shorter events, 0.0 us)
Async XLA Ops:
  26.5 19.8 %copy-start.2 = (bf16[8,64,1024]{2,1,0:T(8,128)(2,1)S(1)}, bf16[8,64,1024]{2,1,0:T(8,128)(2,1)}, u32[]{:S(2)}) copy-start(bf16[8,64,1024]{2,1,0:T(8,128)(2,1)} %get-tuple-element.24) | copy-start | bytes 3145732
  35.9 36.7 %all-to-all-start = ((bf16[32,2,4,16,128]{4,3,2,1,0:T(8,128)(2,1)}), bf16[32,2,4,16,128]{4,3,2,1,0:T(8,128)(2,1)S(1)}, u32[]{:S(2)}, u32[]{:S(2)}) async-start(bf16[32,2,4,16,128]{4,3,2,1,0:T(8,128)(2,1)} %get-tuple-element.22), calls=%async_computation | async-start | bytes 2097152 | tf_op jit(solution)/shard_map/all_to_all | solution.py:479
  48.7 2.2 %copy-start.4 = (bf16[64,512]{1,0:T(8,128)(2,1)S(1)}, bf16[64,512]{1,0:T(8,128)(2,1)}, u32[]{:S(2)}) copy-start(bf16[64,512]{1,0:T(8,128)(2,1)} %param.20) | copy-start | bytes 196612
  52.3 0.9 copy-start.3
  53.4 20.7 %copy-start.5 = (bf16[256,64]{0,1:T(8,128)(2,1)S(1)}, bf16[256,64]{0,1:T(8,128)(2,1)}, u32[]{:S(2)}) copy-start(bf16[256,64]{0,1:T(8,128)(2,1)} %param.21) | copy-start | bytes 98308
  54.6 28.3 %copy-start.6 = (bf16[16,128,128]{2,1,0:T(8,128)(2,1)S(1)}, bf16[16,128,128]{2,1,0:T(8,128)(2,1)}, u32[]{:S(2)}) copy-start(bf16[16,128,128]{2,1,0:T(8,128)(2,1)} %get-tuple-element.29) | copy-start | bytes 1572868
  72.6 1.7 %copy-start = (bf16[32,2,4,16,128]{4,3,2,1,0:T(8,128)(2,1)}, bf16[32,2,4,16,128]{4,3,2,1,0:T(8,128)(2,1)S(1)}, u32[]{:S(2)}) copy-start(bf16[32,2,4,16,128]{4,3,2,1,0:T(8,128)(2,1)S(1)} %all-to-all-done.received_ref) | copy-start | bytes 3145732
  72.6 18.7 %collective-permute-start = (bf16[8,16,2048]{2,1,0:T(8,128)(2,1)S(1)}, bf16[8,16,2048]{2,1,0:T(8,128)(2,1)S(1)}, u32[]{:S(2)}, u32[]{:S(2)}) collective-permute-start(bf16[8,16,2048]{2,1,0:T(8,128)(2,1)S(1)} %convolution_convert_fusion), channel_id=1, source_target_pairs={{0,1},{1,0},{2,3},{3,2},{4,5},{5,4},{6,7},{7,6},{8,9},{9,8},{10,11... | collective-permute-start | bytes 1572872 | tf_op jit(solution)/shard_map/ppermute | solution.py:142
  78.1 21.9 %all-to-all-start.1 = ((bf16[32,4,16,128]{3,2,1,0:T(8,128)(2,1)}), bf16[32,4,16,128]{3,2,1,0:T(8,128)(2,1)S(1)}, u32[]{:S(2)}, u32[]{:S(2)}) async-start(bf16[32,4,16,128]{3,2,1,0:T(8,128)(2,1)} %triangle_product.1), calls=%async_computation.1 | async-start | bytes 1048576 | tf_op jit(solution)/shard_map/all_to_all | solution.py:519
  81.1 10.1 %collective-permute-start.1 = (f32[8,16]{0,1:T(8,128)S(1)}, f32[8,16]{0,1:T(8,128)S(1)}, u32[]{:S(2)}, u32[]{:S(2)}) collective-permute-start(f32[8,16]{0,1:T(8,128)S(1)} %bitcast_reduce_fusion), channel_id=1, source_target_pairs={{0,1},{1,0},{2,3},{3,2},{4,5},{5,4},{6,7},{7,6},{8,9},{9,8},{10,11... | collective-permute-start | bytes 1544 | tf_op jit(solution)/shard_map/ppermute | solution.py:142
  94.2 2.9 %copy-start.7 = (bf16[16,64,64]{2,1,0:T(8,128)(2,1)S(1)}, bf16[16,64,64]{2,1,0:T(8,128)(2,1)}, u32[]{:S(2)}) copy-start(bf16[16,64,64]{2,1,0:T(8,128)(2,1)} %get-tuple-element.30) | copy-start | bytes 393220
  100.0 0.8 copy-start.1
